TPU v7x, 32 devices: a whole 2x2x4 slice. The times are simulated.
32 devices in a mesh: dp: 2 (over x), fsdp: 16 (over z, y, core).
Axes of the slice: x: 2, y: 2, z: 4, core: 2. Of those that a mesh axis runs over, the one named last changes fastest.
Arguments:
- inputs: bfloat16 [32, 788, 768], P(('dp', 'fsdp')), may hold values from -6 to 6
- cotangent: bfloat16 [32, 788, 768], P(('dp', 'fsdp')), may hold values from -6 to 6
- segment_ids: int32 [32, 788], P(('dp', 'fsdp')), may hold values from 0 to 3, as said below
- keep_rows: int32 [32, 788], P(('dp', 'fsdp')), may hold values from 0 to 1, as said below
- index_map: int32 [197, 197], replicated, may hold values from 0 to 731
- ln1_gain: bfloat16 [768], P(('dp', 'fsdp')), may hold values from 0.5 to 1.5
- ln1_bias: bfloat16 [768], P(('dp', 'fsdp')), may hold values from -3 to 3
- qkv_weight: bfloat16 [768, 2304], P(('dp', 'fsdp')), may hold values from -0.21875 to 0.21875
- qv_bias: bfloat16 [2, 768], P(None, ('dp', 'fsdp')), may hold values from -3 to 3
- out_weight: bfloat16 [768, 768], P(None, ('dp', 'fsdp')), may hold values from -1.75 to 1.75
- out_bias: bfloat16 [768], P(('dp', 'fsdp')), may hold values from -2 to 2
- gamma_attn: bfloat16 [768], P(('dp', 'fsdp')), may hold values from 0.5 to 2
- rel_table: bfloat16 [12, 736], P(None, ('dp', 'fsdp')), may hold values from -4 to 4
- ln2_gain: bfloat16 [768], P(('dp', 'fsdp')), may hold values from 0.5 to 1.5
- ln2_bias: bfloat16 [768], P(('dp', 'fsdp')), may hold values from -3 to 3
- fc1_weight: bfloat16 [768, 3072], P(('dp', 'fsdp')), may hold values from -0.21875 to 0.21875
- fc1_bias: bfloat16 [3072], P(('dp', 'fsdp')), may hold values from -3 to 3
- fc2_weight: bfloat16 [3072, 768], P(None, ('dp', 'fsdp')), may hold values from -0.109375 to 0.109375
- fc2_bias: bfloat16 [768], P(('dp', 'fsdp')), may hold values from -2 to 2
- gamma_mlp: bfloat16 [768], P(('dp', 'fsdp')), may hold values from 0.5 to 2
Outputs:
- output: bfloat16 [32, 788, 768], P(('dp', 'fsdp'))
- input_grad: bfloat16 [32, 788, 768], P(('dp', 'fsdp'))
- grad_ln1_gain: float32 [768], P(('dp', 'fsdp'))
- grad_ln1_bias: float32 [768], P(('dp', 'fsdp'))
- grad_qkv_weight: float32 [768, 2304], P(('dp', 'fsdp'))
- grad_qv_bias: float32 [2, 768], P(None, ('dp', 'fsdp'))
- grad_out_weight: float32 [768, 768], P(None, ('dp', 'fsdp'))
- output_bias_gradient: float32 [768], P(('dp', 'fsdp'))
- grad_gamma_attn: float32 [768], P(('dp', 'fsdp'))
- grad_rel_table: float32 [12, 736], P(None, ('dp', 'fsdp'))
- grad_ln2_gain: float32 [768], P(('dp', 'fsdp'))
- grad_ln2_bias: float32 [768], P(('dp', 'fsdp'))
- grad_fc1_weight: float32 [768, 3072], P(('dp', 'fsdp'))
- grad_fc1_bias: float32 [3072], P(('dp', 'fsdp'))
- grad_fc2_weight: float32 [3072, 768], P(None, ('dp', 'fsdp'))
- grad_fc2_bias: float32 [768], P(('dp', 'fsdp'))
- grad_gamma_mlp: float32 [768], P(('dp', 'fsdp'))
Inputs may be any that keep to these rules, and one draw needn't show every extreme that they name: `segment_ids`: each sequence is either 4 runs of 197 rows with segment numbers 0 to 3 in order, or 3 such runs numbered 0 to 2 that follow a run of padding rows and precede another (197 padding rows in all, either run possibly empty); padding rows have segment number 4 - 1. `keep_rows`: 0 exactly on the padding rows described for segment_ids.
All inputs are finite; a program needn't handle non-finite values.
Results may differ from a plain program's by a relative error of at most 0.011.
Values may be sent and summed in bfloat16 or wider, within the bound.
No kernel may reach another device: no remote copies, remote signals or barrier semaphores. Data moves between devices by JAX's collectives and lax.ppermute only.
A program may use at most 128 MiB of HBM per device.

v0:
```python
import functools
import jax
import jax.numpy as jnp
from jax import lax
from jax.experimental import pallas as pl
from jax.experimental.pallas import tpu as pltpu
from jax.sharding import PartitionSpec as P

AX = ("dp", "fsdp")
IMGS = 4
EPS = 1e-06
MASKED = -1e30
ROOT_HALF = 0.7071067811865476
INV_ROOT_TAU = 0.3989422804014327
F32 = jnp.float32
BF16 = jnp.bfloat16
VMEM_LIMIT = 60 * 1024 * 1024

LN1_G, LN1_B, Q_B, V_B, OUT_B, GAM_A, LN2_G, LN2_B, FC2_B, GAM_M = range(10)
FC1_B = 16
TABLE = 32
SMALL = 128
G_LN1_G, G_LN1_B, G_Q_B, G_V_B, G_OUT_B, G_GAM_A, G_LN2_G, G_LN2_B, G_FC2_B, G_GAM_M = range(10)


def nn(a, b):
    return lax.dot_general(a, b, (((1,), (0,)), ((), ())), preferred_element_type=F32)


def nt(a, b):
    return lax.dot_general(a, b, (((1,), (1,)), ((), ())), preferred_element_type=F32)


def tn(a, b):
    return lax.dot_general(a, b, (((0,), (0,)), ((), ())), preferred_element_type=F32)


def full(shape):
    return pl.BlockSpec(shape, lambda *_: (0,) * len(shape))


def cost(gigaflops, megabytes=4):
    return pl.CostEstimate(
        flops=int(gigaflops * 2e7), bytes_accessed=int(megabytes * 2e4), transcendentals=0
    )


def after(value, *others):
    return lax.optimization_barrier((value, others))[0]


def params(grid_rank=1):
    return pltpu.CompilerParams(
        dimension_semantics=("arbitrary",) * grid_rank, vmem_limit_bytes=VMEM_LIMIT
    )


def smem():
    return pl.BlockSpec(memory_space=pltpu.SMEM)


def exchange_orders(count):
    bits = count.bit_length() - 1
    if bits < 3:
        return (list(range(bits)),) * 2
    rest = list(range(2, bits - 1))
    return [0, 1, bits - 1] + rest, [0, bits - 1, 1] + rest[::-1]

def exchange(values, step, count):
    orders = exchange_orders(count)
    return lax.ppermute(values, AX, [(i, i ^ (1 << orders[i & 1][step])) for i in range(count)])


def exchange_owners(count):
    orders = exchange_orders(count)
    bits = len(orders[0])
    me = lax.axis_index(AX)
    spot = jnp.arange(count, dtype=jnp.int32)
    other = spot >> (bits - 1) if bits else spot
    kind = jnp.bitwise_xor(jnp.bitwise_and(me, 1), other)
    flips = other
    for step in range(1, bits):
        bit = jnp.bitwise_and(spot >> (bits - 1 - step), 1)
        flips = jnp.bitwise_or(
            flips, bit << jnp.where(kind == 1, orders[1][step], orders[0][step])
        )
    return jnp.bitwise_xor(me, flips)


def gather_halves(values, count, before):
    for number, step in enumerate(reversed(range(count.bit_length() - 1))):
        got = exchange(values, step, count)
        if number < len(before):
            got = after(got, *before[number])
        if step == 0:
            return values, got
        values = jnp.concatenate([values, got], axis=0)
    half = values.shape[0] // 2
    return values[:half], values[half:]


def scatter_step(pieces, send, step, count, *others):
    got = after(exchange(send, step, count), *others)
    pieces = pieces + [got]
    rows = got.shape[0]
    if step == count.bit_length() - 2:
        return sum(piece[:rows].astype(F32) for piece in pieces), None
    send = sum(piece[rows // 2 : rows].astype(F32) for piece in pieces).astype(BF16)
    return pieces, send


def in_chunks(rows, size, body):
    def one(number, carry):
        body(pl.ds(pl.multiple_of(number * size, 16), size))
        return carry

    lax.fori_loop(0, rows // size, one, 0)


def row_order(column, width):
    rows = column.shape[0]
    return (lax.broadcasted_iota(jnp.int32, (rows, width), 1) == column).astype(BF16)


def block_source(first, number, rows, image, length):
    at = first + image * number + rows
    at = jnp.where(at >= length, at - length, at)
    return jnp.where(rows < image, at, -1)


def place_rows(first, source, target_rows, image):
    length = source.shape[0]

    def one(number):
        rows = lax.broadcasted_iota(jnp.int32, (target_rows, 1), 0)
        wanted = block_source(first, number, rows, image, length)
        columns = lax.broadcasted_iota(jnp.int32, (target_rows, length), 1)
        return nn((columns == wanted).astype(BF16), source)

    return one


def restore_rows(first, blocked, block_rows, image, length):
    lanes = lax.broadcasted_iota(jnp.int32, (1, block_rows), 1)
    wanted = jnp.concatenate(
        [block_source(first, number, lanes, image, length) for number in range(IMGS)], axis=1
    )
    rows = lax.broadcasted_iota(jnp.int32, (length, IMGS * block_rows), 0)
    return nn((rows == wanted).astype(BF16), blocked)


def pack_body(bias_at, table_at, ratio, bias_ref, table_ref, *rest):
    *row_refs, out_ref, rows_s = rest
    own = out_ref.shape[0]
    rows_s[...] = jnp.zeros_like(rows_s)
    at_row = 0
    for ref in row_refs:
        rows_s[at_row : at_row + ref.shape[0], :] = ref[...].astype(F32)
        at_row += ref.shape[0]
    heads, slots = table_ref.shape
    rows_s[table_at : table_at + heads, :slots] = table_ref[...].astype(F32)
    eye = (
        lax.broadcasted_iota(jnp.int32, (own, own), 0)
        == lax.broadcasted_iota(jnp.int32, (own, own), 1)
    ).astype(BF16)
    small = nt(eye, rows_s[...].astype(BF16))
    biases = jnp.broadcast_to(bias_ref[...].astype(F32), (own, own * ratio))
    at = lax.broadcasted_iota(jnp.int32, (own, own * ratio), 1)
    row = lax.broadcasted_iota(jnp.int32, (own, own * ratio), 0)
    lane = lax.broadcasted_iota(jnp.int32, (own, SMALL), 1)
    for number in range(ratio):
        column = jnp.sum(
            jnp.where(at == row * ratio + number, biases, 0.0), axis=1, keepdims=True
        )
        small = small + jnp.where(lane == bias_at + number, column, 0.0)
    out_ref[...] = small.astype(BF16)


def pack(rows, bias, table, bias_at, table_at, ratio):
    own = rows[0].shape[1]
    operands = (bias, table, *rows)
    return pl.pallas_call(
        functools.partial(pack_body, bias_at, table_at, ratio),
        grid=(1,),
        in_specs=[full(value.shape) for value in operands],
        out_specs=full((own, SMALL)),
        out_shape=jax.ShapeDtypeStruct((own, SMALL), BF16),
        scratch_shapes=[pltpu.VMEM((SMALL, own), F32)],
        compiler_params=params(),
        name="pack",
    )(*operands)


def prepare_body(image, block_rows, info, x_ref, cot_ref, xb_ref, cb_ref, normed_ref, inv_ref):
    first = info[0]

    def one(number, carry):
        here = pl.ds(pl.multiple_of(number * block_rows, 16), block_rows)
        values = place_rows(first, x_ref[...], block_rows, image)(number)
        xb_ref[here, :] = values.astype(BF16)
        normed, inverse = normal(values)
        normed_ref[here, :] = normed
        inv_ref[here, :] = jnp.broadcast_to(inverse, (block_rows, 128))
        cb_ref[here, :] = place_rows(first, cot_ref[...], block_rows, image)(number).astype(BF16)
        return carry

    lax.fori_loop(0, IMGS, one, 0)


def prepare(info, x, cot, image, block_rows):
    length, width = x.shape
    rows = IMGS * block_rows
    return pl.pallas_call(
        functools.partial(prepare_body, image, block_rows),
        grid=(1,),
        in_specs=[smem(), full((length, width)), full((length, width))],
        out_specs=[full((rows, width))] * 3 + [full((rows, 128))],
        out_shape=[
            jax.ShapeDtypeStruct((rows, width), BF16),
            jax.ShapeDtypeStruct((rows, width), BF16),
            jax.ShapeDtypeStruct((rows, width), F32),
            jax.ShapeDtypeStruct((rows, 128), F32),
        ],
        compiler_params=params(),
        cost_estimate=cost(4),
        name="prepare",
    )(info, x, cot)


def expand_body(heads, small_ref, index_ref, vec_ref, fc1b_ref, table_ref, entries_s):
    eye = (
        lax.broadcasted_iota(jnp.int32, (SMALL, SMALL), 0)
        == lax.broadcasted_iota(jnp.int32, (SMALL, SMALL), 1)
    ).astype(BF16)
    width = small_ref.shape[0]
    hidden = fc1b_ref.shape[1]
    ratio = hidden // width
    rows = nt(eye, small_ref[...])
    vec_ref[...] = rows[: vec_ref.shape[0]]
    spread = (
        lax.broadcasted_iota(jnp.int32, (width, hidden), 0)
        == lax.broadcasted_iota(jnp.int32, (width, hidden), 1) // ratio
    ).astype(BF16)
    wide = nn(rows[FC1_B : FC1_B + 8].astype(BF16), spread)
    which = lax.broadcasted_iota(jnp.int32, (8, hidden), 1) % ratio
    mine = lax.broadcasted_iota(jnp.int32, (8, hidden), 0)
    total = jnp.sum(jnp.where(which == mine, wide, 0.0), axis=0, keepdims=True)
    fc1b_ref[...] = jnp.broadcast_to(total, fc1b_ref.shape)
    length, lanes = index_ref.shape
    parts = width // 128
    for head in range(heads):
        for part in range(parts):
            entries_s[head * parts + part] = jnp.broadcast_to(
                rows[TABLE + head : TABLE + head + 1, part * 128 : (part + 1) * 128], (8, 128)
            )

    def one(step, carry):
        at = pl.ds(pl.multiple_of(step * 8, 8), 8)
        for half in range(lanes // 128):
            columns = slice(half * 128, (half + 1) * 128)
            index = index_ref[at, columns]
            low = jnp.bitwise_and(index, 127)
            high = jnp.right_shift(index, 7)
            found = [jnp.full((8, 128), MASKED, F32)] * heads
            for part in range(parts):
                chosen = high == part
                for head in range(heads):
                    taken = jnp.take_along_axis(
                        entries_s[head * parts + part], low, axis=1, mode="promise_in_bounds"
                    )
                    found[head] = jnp.where(chosen, taken, found[head])
            for head in range(heads):
                table_ref[head, at, columns] = found[head]
        return carry

    lax.fori_loop(0, length // 8, one, 0)


def expand(small, index, heads, hidden):
    width = small.shape[0]
    length, lanes = index.shape
    return pl.pallas_call(
        functools.partial(expand_body, heads),
        grid=(1,),
        in_specs=[
            full((width, SMALL)),
            full((length, lanes)),
        ],
        out_specs=[full((64, width)), full((8, hidden)), full((heads, length, lanes))],
        out_shape=[
            jax.ShapeDtypeStruct((64, width), F32),
            jax.ShapeDtypeStruct((8, hidden), F32),
            jax.ShapeDtypeStruct((heads, length, lanes), F32),
        ],
        scratch_shapes=[pltpu.VMEM((heads * width // 128, 8, 128), F32)],
        compiler_params=params(),
        cost_estimate=cost(5),
        name="expand",
    )(small, index)


def project_body(
    scale,
    owners,
    normed_ref,
    vec_ref,
    mine_any,
    got_any,
    packed_ref,
    low_ref,
    weight_any,
    weight_s,
    sems,
    out_sem,
):
    step = pl.program_id(0)
    half = mine_any.shape[0]
    width = normed_ref.shape[1]
    keeping = pltpu.make_async_copy(weight_s, weight_any, out_sem)

    @pl.when(step == 0)
    def _():
        copies = []
        for spot in range(2 * half):
            source = mine_any.at[spot] if spot < half else got_any.at[spot - half]
            copy = pltpu.make_async_copy(source, weight_s.at[owners[spot]], sems.at[spot])
            copy.start()
            copies.append(copy)
        low_ref[...] = (
            normed_ref[...] * vec_ref[LN1_G : LN1_G + 1, :] + vec_ref[LN1_B : LN1_B + 1, :]
        ).astype(BF16)
        for copy in copies:
            copy.wait()
        keeping.start()

    bias = jnp.where(
        step == 0,
        vec_ref[Q_B : Q_B + 1, :],
        jnp.where(step == 2, vec_ref[V_B : V_B + 1, :], 0.0),
    )
    columns = pl.ds(pl.multiple_of(step * width, 128), width)
    weight = weight_s[:, :, columns].reshape(width, width)
    result = (nn(low_ref[...], weight) + bias).astype(BF16)
    packed_ref[...] = (result.astype(F32) * jnp.where(step == 0, scale, 1.0)).astype(BF16)

    @pl.when(step == 2)
    def _():
        keeping.wait()


def project(owners, normed, vec, mine, got, head_dim):
    rows, width = normed.shape
    count = owners.shape[0]
    wide = mine.shape[1]
    own = width // count
    anywhere = pl.BlockSpec(memory_space=pl.ANY)
    half = -(-count // 2)
    return pl.pallas_call(
        functools.partial(project_body, head_dim**-0.5),
        grid=(3,),
        in_specs=[smem(), full((rows, width)), full(vec.shape), anywhere, anywhere],
        out_specs=[
            pl.BlockSpec((rows, width), lambda i: (0, i)),
            full((rows, width)),
            anywhere,
        ],
        out_shape=[
            jax.ShapeDtypeStruct((rows, wide), BF16),
            jax.ShapeDtypeStruct((rows, width), BF16),
            jax.ShapeDtypeStruct((count, own, wide), BF16),
        ],
        scratch_shapes=[
            pltpu.VMEM((count, own, wide), BF16),
            pltpu.SemaphoreType.DMA((2 * half,)),
            pltpu.SemaphoreType.DMA,
        ],
        compiler_params=params(),
        cost_estimate=cost(4),
        name="project",
    )(owners, normed, vec, mine.reshape(half, own, wide), got.reshape(half, own, wide))


def turn_body(order_ref, vec_ref, cb_ref, low_ref, up_ref, up_t_ref, low_t_ref):
    up = (vec_ref[GAM_M : GAM_M + 1, :] * cb_ref[...].astype(F32)).astype(BF16)
    up_ref[...] = up
    width = low_ref.shape[1]

    def turned(here):
        order = row_order(order_ref[here, :], width)
        up_t_ref[here, :] = nt(order, up_ref[...]).astype(BF16)
        low_t_ref[here, :] = nt(order, low_ref[...]).astype(BF16)

    in_chunks(width, width // 2, turned)


def turn(order, vec, cb, low):
    rows, width = cb.shape
    return pl.pallas_call(
        turn_body,
        grid=(1,),
        in_specs=[full((width, 1)), full(vec.shape), full((rows, width)), full((rows, width))],
        out_specs=[full((rows, width)), full((width, rows)), full((width, rows))],
        out_shape=[
            jax.ShapeDtypeStruct((rows, width), BF16),
            jax.ShapeDtypeStruct((width, rows), BF16),
            jax.ShapeDtypeStruct((width, rows), BF16),
        ],
        compiler_params=params(),
        cost_estimate=cost(3),
        name="turn",
    )(order, vec, cb, low)


def halves(values):
    lanes = lax.broadcasted_iota(jnp.int32, values.shape, 1)
    zero = jnp.zeros((), values.dtype)
    side = values.shape[1] // 2
    return (jnp.where(lanes < side, values, zero), jnp.where(lanes >= side, values, zero))


def attend_body(block_rows, info, q_ref, k_ref, v_ref, table_ref, mixed_ref, weight_ref):
    rows = lax.broadcasted_iota(jnp.int32, (block_rows, block_rows), 0)
    columns = lax.broadcasted_iota(jnp.int32, (block_rows, block_rows), 1)
    alone = jnp.where(rows == columns, 0.0, MASKED)

    def one(number, carry):
        padded = jnp.logical_and(info[1] == 1, number == IMGS - 1)
        here = pl.ds(pl.multiple_of(number * block_rows, 16), block_rows)
        queries = halves(q_ref[here, :])
        values = halves(v_ref[here, :])
        keys = k_ref[here, :]
        mixed = None
        for side in range(2):
            bias = jnp.where(padded, alone, table_ref[side, :, :block_rows])
            scores = nt(queries[side], keys) + bias
            raised = jnp.exp(scores - jnp.max(scores, axis=1, keepdims=True))
            weights = raised * (1.0 / jnp.sum(raised, axis=1, keepdims=True))
            weight_ref[side, number] = weights
            part = nn(weights.astype(BF16), values[side])
            mixed = part if mixed is None else mixed + part
        mixed_ref[here, :] = mixed.astype(BF16)
        return carry

    lax.fori_loop(0, IMGS, one, 0, unroll=True)


def attend(info, packed, table, block_rows):
    rows, three = packed.shape
    pairs = three // (3 * 128)
    heads, length, lanes = table.shape
    return pl.pallas_call(
        functools.partial(attend_body, block_rows),
        grid=(pairs,),
        in_specs=[
            smem(),
            pl.BlockSpec((rows, 128), lambda p: (0, p)),
            pl.BlockSpec((rows, 128), lambda p: (0, pairs + p)),
            pl.BlockSpec((rows, 128), lambda p: (0, 2 * pairs + p)),
            pl.BlockSpec((2, length, lanes), lambda p: (p, 0, 0)),
        ],
        out_specs=[
            pl.BlockSpec((rows, 128), lambda p: (0, p)),
            pl.BlockSpec((2, IMGS, block_rows, block_rows), lambda p: (p, 0, 0, 0)),
        ],
        out_shape=[
            jax.ShapeDtypeStruct((rows, pairs * 128), BF16),
            jax.ShapeDtypeStruct((heads, IMGS, block_rows, block_rows), F32),
        ],
        compiler_params=params(),
        cost_estimate=cost(6),
        name="attend",
    )(info, packed, packed, packed, table)


def attend_back_body(block_rows, scale, q_ref, k_ref, v_ref, weight_ref, grad_ref, *rest):
    packed_ref, table_ref = rest[-2:]
    for side in range(2):
        table_ref[side] = jnp.zeros(table_ref.shape[1:], F32)

    def one(number, carry):
        here = pl.ds(pl.multiple_of(number * block_rows, 16), block_rows)
        queries = halves(q_ref[here, :])
        keys = halves(k_ref[here, :])
        grads = halves(grad_ref[here, :])
        values = v_ref[here, :]
        dq = dk = dv = 0.0
        for side in range(2):
            weights = weight_ref[side, number]
            up = nt(grads[side], values)
            inner = jnp.sum(weights * up, axis=1, keepdims=True)
            score = (weights * (up - inner)).astype(BF16)
            dv += tn(weights.astype(BF16), grads[side])
            dq += nn(score, keys[side])
            dk += tn(score, queries[side])
            table_ref[side, :, :block_rows] += score.astype(F32)
        packed_ref[0, here, :] = (dq * scale).astype(BF16)
        packed_ref[1, here, :] = dk.astype(BF16)
        packed_ref[2, here, :] = dv.astype(BF16)
        return carry

    lax.fori_loop(0, IMGS, one, 0, unroll=True)


def attend_back(packed, weights, mixed_grad, head_dim, lanes, first, last, earlier=()):
    rows, three = packed.shape
    pairs = three // (3 * 128)
    heads, _, block_rows, _ = weights.shape
    part = pl.BlockSpec((rows, 128), lambda p: (0, first + p))
    return pl.pallas_call(
        functools.partial(attend_back_body, block_rows, head_dim**-0.5),
        grid=(last - first,),
        in_specs=[
            part,
            pl.BlockSpec((rows, 128), lambda p: (0, pairs + first + p)),
            pl.BlockSpec((rows, 128), lambda p: (0, 2 * pairs + first + p)),
            pl.BlockSpec((2, IMGS, block_rows, block_rows), lambda p: (first + p, 0, 0, 0)),
            part,
        ]
        + [pl.BlockSpec(memory_space=pl.ANY)] * len(earlier),
        out_specs=[
            pl.BlockSpec((3, rows, 128), lambda p: (0, 0, first + p)),
            pl.BlockSpec((2, block_rows, lanes), lambda p: (first + p, 0, 0)),
        ],
        out_shape=[
            jax.ShapeDtypeStruct((3, rows, pairs * 128), BF16),
            jax.ShapeDtypeStruct((heads, block_rows, lanes), F32),
        ],
        input_output_aliases={5: 0, 6: 1} if earlier else {},
        compiler_params=params(),
        cost_estimate=cost(4),
        name="attend_back",
    )(packed, packed, packed, weights, mixed_grad, *earlier)


def cumulative(values):
    squared = jnp.exp(-0.5 * values * values)
    size = jnp.abs(values) * ROOT_HALF
    t = 1.0 / (1.0 + 0.3275911 * size)
    poly = t * (
        0.254829592 + t * (-0.284496736 + t * (1.421413741 + t * (-1.453152027 + t * 1.061405429)))
    )
    tail = 0.5 * poly * squared
    return jnp.where(values < 0, tail, 1.0 - tail), squared * INV_ROOT_TAU


def normal(values):
    average = jnp.mean(values, axis=-1, keepdims=True)
    centred = values - average
    inverse = lax.rsqrt(jnp.mean(centred * centred, axis=-1, keepdims=True) + EPS)
    return centred * inverse, inverse


def column_sum(ref, row, values):
    ref[row : row + 1, :] = jnp.sum(values, axis=0, keepdims=True)


class Late:
    def __init__(self, sources, targets, sems):
        self.copies = [
            pltpu.make_async_copy(source, target, sems.at[number])
            for number, (source, target) in enumerate(zip(sources, targets, strict=True))
        ]

    def start(self):
        for copy in self.copies:
            copy.start()

    def wait(self):
        for copy in self.copies:
            copy.wait()


def feed_body(
    image,
    block_rows,
    info,
    order_ref,
    mixed_ref,
    xb_ref,
    up_ref,
    up_t_ref,
    vec_ref,
    bias_ref,
    out_w_ref,
    fc1_ref,
    fc2_ref,
    cb_any,
    out_ref,
    keep_ref,
    send_ref,
    fc1_sum_ref,
    mixed_grad_ref,
    after_grad_ref,
    sums_ref,
    ff_s,
    second_s,
    cb_s,
    after_s,
    branch_s,
    low_s,
    turned_s,
    sems,
):
    step = pl.program_id(0)
    last = pl.num_programs(0) - 1
    rows, width = xb_ref.shape
    late = Late((cb_any,), (cb_s,), sems)

    half = keep_ref.shape[0]

    def put_grads(columns, turned_ref, values):
        def one(here):
            size = here.size
            keep_ref[here, columns] = nn(turned_ref[here, :], values).astype(BF16)
            there = pl.ds(pl.multiple_of(half + here.start, 16), size)
            send_ref[here, columns] = nn(turned_ref[there, :], values).astype(BF16)

        in_chunks(half, half // 2, one)

    def turn_low():
        def turned(here):
            order = row_order(order_ref[here, :], width)
            turned_s[here, :] = nt(order, low_s[...]).astype(BF16)

        in_chunks(width, width // 2, turned)

    @pl.when(step == 0)
    def _():
        late.start()
        ff_s[...] = jnp.zeros_like(ff_s)
        second_s[...] = jnp.zeros_like(second_s)

        def one(here):
            branch = nt(mixed_ref[here, :], out_w_ref[...]) + vec_ref[OUT_B : OUT_B + 1, :]
            branch_s[here, :] = branch
            after_attn = xb_ref[here, :].astype(F32) + vec_ref[GAM_A : GAM_A + 1, :] * branch
            after_s[here, :] = after_attn
            normed, _ = normal(after_attn)
            low_s[here, :] = (
                normed * vec_ref[LN2_G : LN2_G + 1, :] + vec_ref[LN2_B : LN2_B + 1, :]
            ).astype(BF16)

        in_chunks(rows, rows // 2, one)
        turn_low()

    @pl.when(step < last)
    def _():
        tile = fc1_ref.shape[1]
        pre = nn(low_s[...], fc1_ref[...]) + bias_ref[0:1, :]
        phi, density = cumulative(pre)
        hidden = (pre * phi).astype(BF16)
        slope = phi + pre * density
        grad = (nn(up_ref[...], fc2_ref[...]) * slope).astype(BF16)
        ff_s[...] += nt(hidden, fc2_ref[...])
        second_s[...] += nt(grad, fc1_ref[...])
        for columns, values in (
            (slice(0, tile), nn(turned_s[...], grad)),
            (slice(tile, 2 * tile), nn(up_t_ref[...], hidden)),
        ):
            keep_ref[:, columns] = values[:half].astype(BF16)
            send_ref[:, columns] = values[half:].astype(BF16)
        fc1_sum_ref[...] = jnp.broadcast_to(
            jnp.sum(grad.astype(F32), axis=0, keepdims=True), fc1_sum_ref.shape
        )

    @pl.when(step == last)
    def _():
        late.wait()
        cot = cb_s[...].astype(F32)
        sums_ref[...] = jnp.zeros_like(sums_ref)
        normed, inverse = normal(after_s[...])
        second = second_s[...]
        column_sum(sums_ref, G_LN2_G, second * normed)
        column_sum(sums_ref, G_LN2_B, second)
        scaled = second * vec_ref[LN2_G : LN2_G + 1, :]
        inner = jnp.mean(scaled, axis=-1, keepdims=True)
        along = jnp.mean(scaled * normed, axis=-1, keepdims=True)
        after_grad = cot + inverse * (scaled - inner - normed * along)
        after_grad_ref[...] = after_grad
        column_sum(sums_ref, G_GAM_A, after_grad * branch_s[...])
        low = (vec_ref[GAM_A : GAM_A + 1, :] * after_grad).astype(BF16)
        column_sum(sums_ref, G_OUT_B, low.astype(F32))
        mixed_grad_ref[...] = nn(low, out_w_ref[...]).astype(BF16)
        low_s[...] = low
        turn_low()
        put_grads(slice(0, width), turned_s, mixed_ref[...])
        branch = ff_s[...] + vec_ref[FC2_B : FC2_B + 1, :]
        result = (after_s[...] + vec_ref[GAM_M : GAM_M + 1, :] * branch).astype(BF16)
        out_ref[...] = restore_rows(info[0], result, block_rows, image, out_ref.shape[0]).astype(
            BF16
        )
        column_sum(sums_ref, G_GAM_M, cot * branch)
        column_sum(sums_ref, G_FC2_B, up_ref[...].astype(F32))


def feed(
    info,
    order,
    mixed,
    xb,
    up,
    up_t,
    vec,
    fc1b,
    weights,
    cb,
    image,
    block_rows,
    length,
    tile,
):
    rows, width = xb.shape
    hidden = fc1b.shape[1]
    steps = hidden // tile
    anywhere = pl.BlockSpec(memory_space=pl.ANY)
    once = pl.Buffered(1)

    def at(i):
        return jnp.minimum(i, steps - 1)

    def fixed(shape):
        return pl.BlockSpec(shape, lambda i: (0, 0), pipeline_mode=once)

    return pl.pallas_call(
        functools.partial(feed_body, image, block_rows),
        grid=(steps + 1,),
        in_specs=[
            smem(),
            fixed((width, 1)),
            fixed((rows, width)),
            fixed((rows, width)),
            fixed((rows, width)),
            fixed((width, rows)),
            fixed(vec.shape),
            pl.BlockSpec((8, tile), lambda i: (0, at(i))),
            pl.BlockSpec((width, width), lambda i: (0, 2 * hidden // width), pipeline_mode=once),
            pl.BlockSpec((width, tile), lambda i: (0, at(i))),
            pl.BlockSpec((width, tile), lambda i: (0, steps + at(i))),
        ]
        + [anywhere],
        out_specs=[
            full((length, width)),
            pl.BlockSpec((width // 2, 2 * tile), lambda i: (0, i)),
            pl.BlockSpec((width // 2, 2 * tile), lambda i: (0, i)),
            pl.BlockSpec((8, tile), lambda i: (0, at(i))),
            full((rows, width)),
            full((rows, width)),
            full((16, width)),
        ],
        out_shape=[
            jax.ShapeDtypeStruct((length, width), BF16),
            jax.ShapeDtypeStruct((width // 2, 2 * hidden + width), BF16),
            jax.ShapeDtypeStruct((width // 2, 2 * hidden + width), BF16),
            jax.ShapeDtypeStruct((8, hidden), F32),
            jax.ShapeDtypeStruct((rows, width), BF16),
            jax.ShapeDtypeStruct((rows, width), F32),
            jax.ShapeDtypeStruct((16, width), F32),
        ],
        scratch_shapes=[
            pltpu.VMEM((rows, width), F32),
            pltpu.VMEM((rows, width), F32),
            pltpu.VMEM((rows, width), BF16),
            pltpu.VMEM((rows, width), F32),
            pltpu.VMEM((rows, width), F32),
            pltpu.VMEM((rows, width), BF16),
            pltpu.VMEM((width, rows), BF16),
            pltpu.SemaphoreType.DMA((1,)),
        ],
        compiler_params=params(),
        cost_estimate=cost(28),
        name="feed",
    )(
        info,
        order,
        mixed,
        xb,
        up,
        up_t,
        vec,
        fc1b,
        weights,
        weights,
        weights,
        cb,
    )


def weight_grad_body(low_t_ref, packed_ref, keep_ref, send_ref):
    half = keep_ref.shape[0]
    keep_ref[...] = nn(low_t_ref[:half], packed_ref[...]).astype(BF16)
    send_ref[...] = nn(low_t_ref[half:], packed_ref[...]).astype(BF16)


def weight_grad(low_t, packed_grad):
    width, rows = low_t.shape
    return pl.pallas_call(
        weight_grad_body,
        grid=(3,),
        in_specs=[full((width, rows)), pl.BlockSpec((None, rows, width), lambda i: (i, 0, 0))],
        out_specs=[pl.BlockSpec((width // 2, width), lambda i: (0, i))] * 2,
        out_shape=[jax.ShapeDtypeStruct((width // 2, 3 * width), BF16)] * 2,
        compiler_params=params(),
        cost_estimate=cost(5),
        name="weight_grad",
    )(low_t, packed_grad)


def input_grad_body(
    image,
    block_rows,
    info,
    packed_ref,
    weight_ref,
    vec_ref,
    normed_any,
    inv_any,
    after_grad_any,
    out_ref,
    sums_ref,
    first_s,
    normed_s,
    inv_s,
    after_grad_s,
    sems,
):
    step = pl.program_id(0)
    late = Late((normed_any, inv_any, after_grad_any), (normed_s, inv_s, after_grad_s), sems)

    @pl.when(step == 0)
    def _():
        late.start()
        first_s[...] = jnp.zeros_like(first_s)
        sums_ref[...] = jnp.zeros_like(sums_ref)
        column_sum(sums_ref, G_Q_B, packed_ref[...].astype(F32))

    def one(here):
        first_s[here, :] += nt(packed_ref[here, :], weight_ref[...])

    in_chunks(first_s.shape[0], first_s.shape[0] // 2, one)

    @pl.when(step == 2)
    def _():
        late.wait()
        column_sum(sums_ref, G_V_B, packed_ref[...].astype(F32))
        first = first_s[...]
        normed = normed_s[...]
        column_sum(sums_ref, G_LN1_G, first * normed)
        column_sum(sums_ref, G_LN1_B, first)
        scaled = first * vec_ref[LN1_G : LN1_G + 1, :]
        inner = jnp.mean(scaled, axis=-1, keepdims=True)
        along = jnp.mean(scaled * normed, axis=-1, keepdims=True)
        back = inv_s[:, :1] * (scaled - inner - normed * along)
        result = (after_grad_s[...] + back).astype(BF16)
        out_ref[...] = restore_rows(info[0], result, block_rows, image, out_ref.shape[0]).astype(
            BF16
        )


def input_grad(info, packed_grad, weights, vec, normed, inv, after_grad, image, block_rows, length):
    rows, width = normed.shape
    anywhere = pl.BlockSpec(memory_space=pl.ANY)
    return pl.pallas_call(
        functools.partial(input_grad_body, image, block_rows),
        grid=(3,),
        in_specs=[
            smem(),
            pl.BlockSpec((None, rows, width), lambda i: (i, 0, 0)),
            pl.BlockSpec((width, width), lambda i: (0, i)),
            full(vec.shape),
            anywhere,
            anywhere,
            anywhere,
        ],
        out_specs=[full((length, width)), full((16, width))],
        out_shape=[
            jax.ShapeDtypeStruct((length, width), BF16),
            jax.ShapeDtypeStruct((16, width), F32),
        ],
        scratch_shapes=[
            pltpu.VMEM((rows, width), F32),
            pltpu.VMEM((rows, width), F32),
            pltpu.VMEM((rows, 128), F32),
            pltpu.VMEM((rows, width), F32),
            pltpu.SemaphoreType.DMA((3,)),
        ],
        compiler_params=params(),
        cost_estimate=cost(8),
        name="input_grad",
    )(info, packed_grad, weights, vec, normed, inv, after_grad)


def table_grad_body(heads, groups, table_ref, index_ref, out_ref, acc):
    lanes = index_ref.shape[1]
    parts = out_ref.shape[1] // 128
    acc[...] = jnp.zeros_like(acc)
    slots = lax.broadcasted_iota(jnp.int32, (128, lanes), 0).astype(F32).astype(BF16)
    one_bf, zero_bf = jnp.ones((), BF16), jnp.zeros((), BF16)
    zero = jnp.zeros((), BF16)
    group = 8

    def one(step, carry):
        at = pl.ds(pl.multiple_of(step * group, group), group)
        indices = index_ref[at, :]
        lows = jnp.bitwise_and(indices, 127).astype(F32)
        highs = jnp.right_shift(indices, 7).astype(F32)
        values = table_ref[:, at, :]
        left, right = [], []
        for row in range(group):
            low = jnp.broadcast_to(lows[row : row + 1, :], (16, lanes)).astype(BF16)
            high = jnp.broadcast_to(highs[row : row + 1, :], (16, lanes)).astype(BF16)
            right.append(
                jnp.concatenate(
                    [
                        jnp.where(slots[start : start + 16] == low, one_bf, zero_bf)
                        for start in range(0, 128, 16)
                    ],
                    axis=0,
                )
            )
            here = jnp.concatenate(
                [values[:, row, :], jnp.zeros((16 - heads, lanes), F32)], axis=0
            )
            coarse = here.astype(BF16)
            fine = (here - coarse.astype(F32)).astype(BF16)
            masks = [high == jnp.asarray(part, BF16) for part in range(parts)]
            left.append(
                jnp.concatenate(
                    [jnp.where(mask, kind, zero) for kind in (coarse, fine) for mask in masks],
                    axis=0,
                )
            )
        acc[...] += nt(jnp.concatenate(left, axis=1), jnp.concatenate(right, axis=1))
        return carry

    lax.fori_loop(groups[0], groups[1], one, 0)
    half = parts * 16
    for part in range(parts):
        out_ref[:, part * 128 : (part + 1) * 128] = (
            acc[part * 16 : (part + 1) * 16, :] + acc[half + part * 16 : half + (part + 1) * 16, :]
        )


def table_grad(table, index, slots, groups):
    heads, length, lanes = table.shape
    return pl.pallas_call(
        functools.partial(table_grad_body, heads, groups),
        grid=(1,),
        in_specs=[full(table.shape), full(index.shape)],
        out_specs=full((16, slots)),
        out_shape=jax.ShapeDtypeStruct((16, slots), F32),
        scratch_shapes=[pltpu.VMEM((2 * 16 * slots // 128, 128), F32)],
        compiler_params=params(),
        cost_estimate=cost(8),
        name="table_grad",
    )(table, index)


def local(
    inputs,
    cotangent,
    segment_ids,
    keep_rows,
    index_map,
    ln1_gain,
    ln1_bias,
    qkv_weight,
    qv_bias,
    out_weight,
    out_bias,
    gamma_attn,
    rel_table,
    ln2_gain,
    ln2_bias,
    fc1_weight,
    fc1_bias,
    fc2_weight,
    fc2_bias,
    gamma_mlp,
):
    _, length, width = inputs.shape
    heads, per_device = rel_table.shape
    head_dim = width // heads
    own = ln1_gain.shape[0]
    count = width // own
    hidden = fc1_weight.shape[1]
    image = index_map.shape[0]
    block_rows = -(-image // 16) * 16

    keep = keep_rows[0] == 1
    ids = lax.iota(jnp.int32, length)
    info = jnp.stack([jnp.min(jnp.where(keep, ids, length)), jnp.max(jnp.where(keep, 0, 1))])
    moved = index_map // per_device * own + index_map % per_device
    moved = jnp.pad(moved, ((0, block_rows - image), (0, 256 - image)), constant_values=-1)

    small_rows = [
        ln1_gain[None],
        ln1_bias[None],
        qv_bias,
        out_bias[None],
        gamma_attn[None],
        ln2_gain[None],
        ln2_bias[None],
        fc2_bias[None],
        gamma_mlp[None],
    ]
    owners = exchange_owners(count)
    order = (owners[:, None] * own + jnp.arange(own, dtype=jnp.int32)).reshape(-1, 1)
    later = lax.all_gather(
        jnp.concatenate([fc1_weight, fc2_weight.T, out_weight.T], axis=1), AX, axis=0, tiled=True
    )
    xb, cb, normed, inv = prepare(info, inputs[0], cotangent[0], image, block_rows)
    small = pack(small_rows, fc1_bias[None], rel_table, FC1_B, TABLE, hidden // width)
    small = jnp.broadcast_to(after(small, xb)[None], (count, own, SMALL))
    small = lax.all_to_all(small, AX, 0, 0, tiled=True).reshape(width, SMALL)
    vec, fc1b, table = expand(small, moved, heads, hidden)
    mine, got = gather_halves(qkv_weight, count, [(xb,), (small,), (table,)])
    packed, low, qkv_full = project(owners, normed, vec, mine, got, head_dim)
    qkv_full = qkv_full.reshape(width, -1)
    mixed, weights = attend(info, packed, table, block_rows)
    up, up_t, low_t = turn(order, vec, after(cb, mixed), low)
    tile = 512
    out, feed_keep, feed_send, fc1_sum, mixed_grad, after_grad, sums2 = feed(
        info,
        order,
        mixed,
        xb,
        up,
        up_t,
        vec,
        fc1b,
        later,
        cb,
        image,
        block_rows,
        length,
        tile,
    )
    pairs = heads // 2
    some = attend_back(packed, weights, mixed_grad, head_dim, 256, 0, pairs // 2)
    a_pieces, a_send = scatter_step([feed_keep], feed_send, 0, count, some[0])
    packed_grad, table_sum = attend_back(
        packed, weights, after(mixed_grad, a_send), head_dim, 256, pairs // 2, pairs, some
    )
    qkv_keep, qkv_send = weight_grad(low_t, packed_grad)
    in_grad, sums1 = input_grad(
        info,
        packed_grad,
        qkv_full,
        vec,
        normed,
        after(inv, qkv_keep),
        after_grad,
        image,
        block_rows,
        length,
    )
    groups = -(-image // 8)
    slots = own * count
    b_pieces, b_send = scatter_step([qkv_keep], qkv_send, 0, count, in_grad)
    slot_sums = table_grad(after(table_sum, b_send), moved, slots, (0, groups // 2))
    a_pieces, a_send = scatter_step(a_pieces, a_send, 1, count, slot_sums)
    more_sums = table_grad(after(table_sum, a_send), moved, slots, (groups // 2, groups))
    b_pieces, b_send = scatter_step(b_pieces, b_send, 1, count, more_sums)
    a_pieces, a_send = scatter_step(a_pieces, a_send, 2, count, b_send)
    slot_sums = slot_sums + after(more_sums, a_send)

    rows = jnp.concatenate([sums1[:10] + sums2[:10], slot_sums[:heads]], axis=0)
    rows = jnp.transpose(rows.reshape(-1, count, own), (1, 0, 2))
    biases = fc1_sum[0].reshape(count, -1, own)
    swapped = lax.all_to_all(jnp.concatenate([rows, biases], axis=1), AX, 0, 0, tiled=True)
    b_pieces, b_send = scatter_step(b_pieces, b_send, 2, count, swapped)
    for step in range(3, count.bit_length() - 1):
        a_pieces, a_send = scatter_step(a_pieces, a_send, step, count, b_pieces)
        b_pieces, b_send = scatter_step(b_pieces, b_send, step, count, a_pieces)
    feed_wide, qkv_shard = a_pieces, b_pieces
    small_shard = jnp.sum(swapped, axis=0)

    pieces = feed_wide[:, : 2 * hidden].reshape(own, hidden // tile, 2, tile)
    grad_fc1 = pieces[:, :, 0].reshape(own, hidden)
    grad_fc2 = pieces[:, :, 1].reshape(own, hidden).T
    grad_out = feed_wide[:, 2 * hidden :].T
    grad_table = small_shard[10 : 10 + heads, :per_device]
    grad_fc1_bias = small_shard[10 + heads :].reshape(-1)
    return (
        out[None],
        in_grad[None],
        small_shard[G_LN1_G],
        small_shard[G_LN1_B],
        qkv_shard,
        small_shard[G_Q_B : G_V_B + 1],
        grad_out,
        small_shard[G_OUT_B],
        small_shard[G_GAM_A],
        grad_table,
        small_shard[G_LN2_G],
        small_shard[G_LN2_B],
        grad_fc1,
        grad_fc1_bias,
        grad_fc2,
        small_shard[G_FC2_B],
        small_shard[G_GAM_M],
    )


def solution(mesh):
    rows = P(AX)
    columns = P(None, AX)
    return jax.shard_map(
        local,
        mesh=mesh,
        in_specs=(
            rows,
            rows,
            rows,
            rows,
            P(),
            rows,
            rows,
            rows,
            columns,
            columns,
            rows,
            rows,
            columns,
            rows,
            rows,
            rows,
            rows,
            columns,
            rows,
            rows,
        ),
        out_specs=(
            rows,
            rows,
            rows,
            rows,
            rows,
            columns,
            columns,
            rows,
            rows,
            columns,
            rows,
            rows,
            rows,
            rows,
            columns,
            rows,
            rows,
        ),
        check_vma=False,
    )
```

profile of v0, /device:TPU:0, one launch (start us, length us, event | category | flops | bytes accessed | tf_op | source)
XLA Modules:
  0.0 290.0 jit_solution(3645411263238936366)
XLA Ops:
  7.2 1.8 pad_maximum_fusion.3
  9.0 4.1 %collective-permute-start = (bf16[24,2304]{1,0:T(8,128)(2,1)}, bf16[24,2304]{1,0:T(8,128)(2,1)S(1)}, u32[]{:S(2)}, u32[]{:S(2)}) collective-permute-start(bf16[24,2304]{1,0:T(8,128)(2,1)} %param.26), channel_id=1, source_target_pairs={{0,8},{1,5},{2,10},{3,7},{4,12},{5,1},{6,14},{7,3},{8,0},{9,13},{1... | collective-permute-start | bytes 331784 | tf_op jit(solution)/shard_map/ppermute | solution.py:71
  13.1 1.6 pack.1
  14.7 0.7 compare_reduce_fusion
  15.4 0.6 select_reduce_fusion.1
  16.0 1.9 pad_add_fusion.info
  17.9 7.3 %prepare.1 = (bf16[832,768]{1,0:T(8,128)(2,1)}, bf16[832,768]{1,0:T(8,128)(2,1)}, f32[832,768]{1,0:T(8,128)}, f32[832,128]{1,0:T(8,128)}) custom-call(s32[2]{0:T(128)} %pad_add_fusion.info, bf16[788,768]{1,0:T(8,128)(2,1)} %bitcast.40, bf16[788,768]{1,0:T(8,128)(2,1)} %bitcast.41), custom_call_target="tpu_custom_call" | custom-call | flops 80000000 | bytes 80000 | tf_op jit(solution)/shard_map/prepare/pallas_call | solution.py:213
  25.2 0.7 broadcast_in_dim.72
  25.9 3.8 %all-to-all-start = ((bf16[32,24,128]{2,1,0:T(8,128)(2,1)}), bf16[32,24,128]{2,1,0:T(8,128)(2,1)S(1)}, u32[]{:S(2)}, u32[]{:S(2)}) async-start(bf16[32,24,128]{2,1,0:T(8,128)(2,1)} %broadcast_in_dim.72), calls=%async_computation | async-start | bytes 393216 | tf_op jit(solution)/shard_map/all_to_all | solution.py:1014
  29.8 1.8 collective-permute-start.1
  31.6 9.0 %collective-permute-done.1 = bf16[48,2304]{1,0:T(8,128)(2,1)S(1)} collective-permute-done((bf16[48,2304]{1,0:T(8,128)(2,1)S(1)}, bf16[48,2304]{1,0:T(8,128)(2,1)S(1)}, u32[]{:S(2)}, u32[]{:S(2)}) %collective-permute-start.1) | collective-permute-done | bytes 221216 | tf_op jit(solution)/shard_map/ppermute | solution.py:71
  40.6 1.4 all-to-all-done
  42.9 0.7 pad.4.index_ref
  43.6 9.0 %expand.1 = (f32[64,768]{1,0:T(8,128)}, f32[8,3072]{1,0:T(8,128)}, f32[12,208,256]{2,1,0:T(8,128)}) custom-call(bf16[768,128]{1,0:T(8,128)(2,1)} %bitcast.42, s32[208,256]{1,0:T(8,128)} %pad.4.index_ref), custom_call_target="tpu_custom_call" | custom-call | flops 100000000 | bytes 80000 | tf_op jit(solution)/shard_map/expand/pallas_call | solution.py:282
  52.6 6.9 %collective-permute-done.2 = bf16[96,2304]{1,0:T(8,128)(2,1)S(1)} collective-permute-done((bf16[96,2304]{1,0:T(8,128)(2,1)S(1)}, bf16[96,2304]{1,0:T(8,128)(2,1)S(1)}, u32[]{:S(2)}, u32[]{:S(2)}) %collective-permute-start.2) | collective-permute-done | bytes 442400 | tf_op jit(solution)/shard_map/ppermute | solution.py:71
  59.7 12.9 %collective-permute-done.3 = bf16[192,2304]{1,0:T(8,128)(2,1)S(1)} collective-permute-done((bf16[192,2304]{1,0:T(8,128)(2,1)S(1)}, bf16[192,2304]{1,0:T(8,128)(2,1)S(1)}, u32[]{:S(2)}, u32[]{:S(2)}) %collective-permute-start.3) | collective-permute-done | bytes 884768 | tf_op jit(solution)/shard_map/ppermute | solution.py:71
  73.6 0.9 add.173.order_ref
  74.5 4.6 %collective-permute-done.4 = bf16[384,2304]{1,0:T(8,128)(2,1)S(1)} collective-permute-done((bf16[384,2304]{1,0:T(8,128)(2,1)S(1)}, bf16[384,2304]{1,0:T(8,128)(2,1)S(1)}, u32[]{:S(2)}, u32[]{:S(2)}) %collective-permute-start.4) | collective-permute-done | bytes 1769504 | tf_op jit(solution)/shard_map/ppermute | solution.py:71
  79.1 1.2 copy-done.2
  80.3 9.2 %project.1 = (bf16[832,2304]{1,0:T(8,128)(2,1)}, bf16[832,768]{1,0:T(8,128)(2,1)}, bf16[32,24,2304]{2,1,0:T(8,128)(2,1)}) custom-call(s32[32]{0:T(128)} %get-tuple-element.164.owners, f32[832,768]{1,0:T(8,128)} %get-tuple-element.67.normed_ref.normed_any, f32[64,768]{1,0:T(8,128)} %get-tuple-element.70.vec_ref, bf16[16,24,2304]{2,1,0:T(8,128)(2,1)} %bitcast.34, ...), custom_call_target="tpu_custom_call" | custom-call | flops 80000000 | bytes 80000 | tf_op jit(solution)/shard_map/project/pallas_call | solution.py:358
  89.5 11.6 %attend.1 = (bf16[832,768]{1,0:T(8,128)(2,1)}, f32[12,4,208,208]{3,2,1,0:T(8,128)}) custom-call(s32[2]{0:T(128)} %pad_add_fusion.info, bf16[832,2304]{1,0:T(8,128)(2,1)} %get-tuple-element.75.q_ref.k_ref.v_ref, bf16[832,2304]{1,0:T(8,128)(2,1)} %get-tuple-element.75.q_ref.k_ref.v_ref, bf16[832,2304]{1,0:T(8,128)(2,1)} %get-tuple-element.75.q_ref.k_ref.v_ref, ...), custom_call_target="tpu_custom_call" | custom-call | flops 120000000 | bytes 80000 | tf_op jit(solution)/shard_map/attend/pallas_call | solution.py:451
  101.1 6.3 %turn.1 = (bf16[832,768]{1,0:T(8,128)(2,1)}, bf16[768,832]{1,0:T(8,128)(2,1)}, bf16[768,832]{1,0:T(8,128)(2,1)}) custom-call(s32[768,1]{1,0:T(8,128)} %add.173.order_ref, f32[64,768]{1,0:T(8,128)} %get-tuple-element.70.vec_ref, bf16[832,768]{1,0:T(8,128)(2,1)} %get-tuple-element.78.cb_ref.cb_any, bf16[832,768]{1,0:T(8,128)(2,1)} %get-tuple-element.79.low_ref), custom_call_target="tpu_custom_call" | custom-call | flops 60000000 | bytes 80000 | tf_op jit(solution)/shard_map/turn/pallas_call | solution.py:398
  107.4 2.1 all-gather.2.cloned.1.call-done.out_w_ref.fc1_ref.fc2_ref
  109.5 52.7 %feed.1 = (bf16[788,768]{1,0:T(8,128)(2,1)}, bf16[384,6912]{1,0:T(8,128)(2,1)}, bf16[384,6912]{1,0:T(8,128)(2,1)}, f32[8,3072]{1,0:T(8,128)}, bf16[832,768]{1,0:...) custom-call(s32[2]{0:T(128)} %pad_add_fusion.info, s32[768,1]{1,0:T(8,128)} %add.173.order_ref, ...), custom_call_target="tpu_custom_call" | custom-call | flops 560000000 | bytes 80000 | tf_op jit(solution)/shard_map/feed/pallas_call | solution.py:724
  162.4 8.4 %attend_back.2 = (bf16[3,832,768]{2,1,0:T(8,128)(2,1)}, f32[12,208,256]{2,1,0:T(8,128)}) custom-call(bf16[832,2304]{1,0:T(8,128)(2,1)} %get-tuple-element.75.q_ref.k_ref.v_ref, bf16[832,2304]{1,0:T(8,128)(2,1)} %get-tuple-element.75.q_ref.k_ref.v_ref, bf16[832,2304]{1,0:T(8,128)(2,1)} %get-tuple-element.75.q_ref.k_ref.v_ref, ...), custom_call_target="tpu_custom_call" | custom-call | flops 80000000 | bytes 80000 | tf_op jit(solution)/shard_map/attend_back/pallas_call | solution.py:509
  171.3 4.6 %add_convert_fusion = bf16[192,6912]{1,0:T(8,128)(2,1)} fusion(bf16[384,6912]{1,0:T(8,128)(2,1)} %collective-permute-done.5, bf16[384,6912]{1,0:T(8,128)(2,1)} %get-tuple-element.86), kind=kLoop, calls=%fused_computation | loop fusion | flops 5308416 | bytes 7962624 | tf_op jit(solution)/shard_map/convert_element_type | solution.py:108
  175.9 1.5 collective-permute-start.7
  177.4 8.4 %attend_back.3 = (bf16[3,832,768]{2,1,0:T(8,128)(2,1)}, f32[12,208,256]{2,1,0:T(8,128)}) custom-call(bf16[832,2304]{1,0:T(8,128)(2,1)} %get-tuple-element.75.q_ref.k_ref.v_ref, bf16[832,2304]{1,0:T(8,128)(2,1)} %get-tuple-element.75.q_ref.k_ref.v_ref, ...), custom_call_target="tpu_custom_call", output_to_operand_aliasing={{0}: (5, {}), {1}: (6, {})} | custom-call | flops 80000000 | bytes 80000 | tf_op jit(solution)/shard_map/attend_back/pallas_call | solution.py:509
  185.8 6.9 %weight_grad.1 = (bf16[384,2304]{1,0:T(8,128)(2,1)}, bf16[384,2304]{1,0:T(8,128)(2,1)}) custom-call(bf16[768,832]{1,0:T(8,128)(2,1)} %get-tuple-element.95.low_t_ref, bf16[3,832,768]{2,1,0:T(8,128)(2,1)} %get-tuple-element.92.packed_ref), custom_call_target="tpu_custom_call" | custom-call | flops 100000000 | bytes 80000 | tf_op jit(solution)/shard_map/weight_grad/pallas_call | solution.py:796
  192.7 10.6 %input_grad.1 = (bf16[788,768]{1,0:T(8,128)(2,1)}, f32[16,768]{1,0:T(8,128)}) custom-call(s32[2]{0:T(128)} %pad_add_fusion.info, bf16[3,832,768]{2,1,0:T(8,128)(2,1)} %get-tuple-element.92.packed_ref, bf16[768,2304]{1,0:T(8,128)(2,1)} %bitcast.33, f32[64,768]{1,0:T(8,128)} %get-tuple-element.70.vec_ref, f32[832,768]{1,0:T(8,128)} %get-tuple-element.67.normed_ref.normed_any, ...), custom_call_target="tpu_custom_call" | custom-call | flops 160000000 | bytes 80000 | tf_op jit(solution)/shard_map/input_grad/pallas_call | solution.py:862
  203.3 2.6 add_convert_fusion.2
  206.4 7.1 %table_grad.2 = f32[16,768]{1,0:T(8,128)} custom-call(f32[12,208,256]{2,1,0:T(8,128)} %get-tuple-element.107.table_ref, s32[208,256]{1,0:T(8,128)} %pad.4.index_ref), custom_call_target="tpu_custom_call" | custom-call | flops 160000000 | bytes 80000 | tf_op jit(solution)/shard_map/table_grad/pallas_call | solution.py:945
  213.5 3.3 %add_convert_fusion.1 = bf16[96,6912]{1,0:T(8,128)(2,1)} fusion(bf16[192,6912]{1,0:T(8,128)(2,1)S(1)} %collective-permute-done.7, bf16[384,6912]{1,0:T(8,128)(2,1)} %collective-permute-done.5, bf16[384,6912]{1,0:T(8,128)(2,1)} %get-tuple-element.86), kind=kLoop, calls=%fused_computation.1 | loop fusion | flops 3981312 | bytes 5308416 | tf_op jit(solution)/shard_map/convert_element_type | solution.py:108
  216.8 1.5 collective-permute-start.8
  218.3 0.9 slice_reduce_fusion.10
  219.2 0.8 reshape_squeeze.9
  219.9 1.5 copy.55
  221.4 0.8 slice_add_fusion.1
  222.2 7.5 %table_grad.3 = f32[16,768]{1,0:T(8,128)} custom-call(f32[12,208,256]{2,1,0:T(8,128)} %get-tuple-element.107.table_ref, s32[208,256]{1,0:T(8,128)} %pad.4.index_ref), custom_call_target="tpu_custom_call" | custom-call | flops 160000000 | bytes 80000 | tf_op jit(solution)/shard_map/table_grad/pallas_call | solution.py:945
  229.8 2.4 add_convert_fusion.4
  232.8 2.2 collective-permute-done.8
  234.9 2.6 add_convert_fusion.3
  237.6 0.6 pad_maximum_fusion.5
  238.2 1.1 reshape.118
  239.3 0.9 pad_maximum_fusion.2
  240.5 0.9 reshape.139
  241.5 3.1 %all-to-all-start.1 = ((f32[32,1,624]{2,1,0:T(1,128)}), f32[32,1,624]{2,1,0:T(1,128)S(1)}, u32[]{:S(2)}, u32[]{:S(2)}) async-start(f32[32,1,624]{2,1,0:T(1,128)} %reshape.139), calls=%async_computation.1 | async-start | bytes 163840 | tf_op jit(solution)/shard_map/all_to_all | solution.py:1070
  244.6 1.8 collective-permute-start.12
  246.4 6.0 %all-to-all-done.1 = f32[32,1,624]{2,1,0:T(1,128)S(1)} async-done(((f32[32,1,624]{2,1,0:T(1,128)}), f32[32,1,624]{2,1,0:T(1,128)S(1)}, u32[]{:S(2)}, u32[]{:S(2)}) %all-to-all-start.1) | async-done | bytes 79904 | tf_op jit(solution)/shard_map/all_to_all | solution.py:1070
  252.9 0.8 reduce.26
  254.2 1.4 add_convert_fusion.6
  255.8 0.7 copy.59
  257.7 0.8 slice_reduce_fusion.2
  258.6 4.2 %collective-permute-done.12 = bf16[48,6912]{1,0:T(8,128)(2,1)} collective-permute-done((bf16[48,6912]{1,0:T(8,128)(2,1)}, bf16[48,6912]{1,0:T(8,128)(2,1)}, u32[]{:S(2)}, u32[]{:S(2)}) %collective-permute-start.12) | collective-permute-done | bytes 663584 | tf_op jit(solution)/shard_map/ppermute | solution.py:71
  262.8 1.5 add_convert_fusion.5
  264.3 3.2 %collective-permute-start.14 = (bf16[24,6912]{1,0:T(8,128)(2,1)S(1)}, bf16[24,6912]{1,0:T(8,128)(2,1)S(1)}, u32[]{:S(2)}, u32[]{:S(2)}) collective-permute-start(bf16[24,6912]{1,0:T(8,128)(2,1)S(1)} %add_convert_fusion.5), channel_id=1, source_target_pairs={{0,8},{1,5},{2,10},{3,7},{4,12},{5,1},{6,14},{7,3},{8,0},{9,13},{1... | collective-permute-start | bytes 995336 | tf_op jit(solution)/shard_map/ppermute | solution.py:71
  267.5 1.1 add_convert_fusion.7
  268.6 3.1 %collective-permute-start.13 = (bf16[24,2304]{1,0:T(8,128)(2,1)S(1)}, bf16[24,2304]{1,0:T(8,128)(2,1)S(1)}, u32[]{:S(2)}, u32[]{:S(2)}) collective-permute-start(bf16[24,2304]{1,0:T(8,128)(2,1)S(1)} %add_convert_fusion.7), channel_id=1, source_target_pairs={{0,8},{1,5},{2,10},{3,7},{4,12},{5,1},{6,14},{7,3},{8,0},{9,13},{1... | collective-permute-start | bytes 331784 | tf_op jit(solution)/shard_map/ppermute | solution.py:71
  271.8 3.4 %collective-permute-done.14 = bf16[24,6912]{1,0:T(8,128)(2,1)S(1)} collective-permute-done((bf16[24,6912]{1,0:T(8,128)(2,1)S(1)}, bf16[24,6912]{1,0:T(8,128)(2,1)S(1)}, u32[]{:S(2)}, u32[]{:S(2)}) %collective-permute-start.14) | collective-permute-done | bytes 331808 | tf_op jit(solution)/shard_map/ppermute | solution.py:71
  275.2 1.5 convert_add_fusion
  277.9 1.6 slice_reduce_fusion
  279.5 0.9 copy.61
  280.4 0.9 copy.60
  281.3 1.8 convert_add_fusion.1
  (60 shorter events, 7.9 us)
Async XLA Ops:
  7.2 102.3 %all-gather.2.cloned.1.call-start = ((), (), s32[]{:S(2)}) async-start(), calls=%async_computation.2 | async-start | bytes 10948608 | tf_op jit(solution)/shard_map/all_gather | solution.py:1008
  9.0 20.8 %copy-start.1 = (bf16[24,2304]{1,0:T(8,128)(2,1)S(1)}, bf16[24,2304]{1,0:T(8,128)(2,1)}, u32[]{:S(2)}) copy-start(bf16[24,2304]{1,0:T(8,128)(2,1)} %param.26) | copy-start | bytes 331780
  9.0 20.7 %collective-permute-start = (bf16[24,2304]{1,0:T(8,128)(2,1)}, bf16[24,2304]{1,0:T(8,128)(2,1)S(1)}, u32[]{:S(2)}, u32[]{:S(2)}) collective-permute-start(bf16[24,2304]{1,0:T(8,128)(2,1)} %param.26), channel_id=1, source_target_pairs={{0,8},{1,5},{2,10},{3,7},{4,12},{5,1},{6,14},{7,3},{8,0},{9,13},{1... | collective-permute-start | bytes 331784 | tf_op jit(solution)/shard_map/ppermute | solution.py:71
  14.7 10.5 %copy-start.8 = (bf16[24,128]{1,0:T(8,128)(2,1)S(1)}, bf16[24,128]{1,0:T(8,128)(2,1)}, u32[]{:S(2)}) copy-start(bf16[24,128]{1,0:T(8,128)(2,1)} %pack.1) | copy-start | bytes 18436
  17.9 24.7 %copy-start.5 = (s32[197,197]{1,0:T(8,128)S(1)}, s32[197,197]{1,0:T(8,128)}, u32[]{:S(2)}) copy-start(s32[197,197]{1,0:T(8,128)} %param.23) | copy-start | bytes 465712
  25.9 16.1 %all-to-all-start = ((bf16[32,24,128]{2,1,0:T(8,128)(2,1)}), bf16[32,24,128]{2,1,0:T(8,128)(2,1)S(1)}, u32[]{:S(2)}, u32[]{:S(2)}) async-start(bf16[32,24,128]{2,1,0:T(8,128)(2,1)} %broadcast_in_dim.72), calls=%async_computation | async-start | bytes 393216 | tf_op jit(solution)/shard_map/all_to_all | solution.py:1014
  29.8 10.8 %collective-permute-start.1 = (bf16[48,2304]{1,0:T(8,128)(2,1)S(1)}, bf16[48,2304]{1,0:T(8,128)(2,1)S(1)}, u32[]{:S(2)}, u32[]{:S(2)}) collective-permute-start(bf16[48,2304]{1,0:T(8,128)(2,1)S(1)} %pad_maximum_fusion.4), channel_id=1, source_target_pairs={{0,4},{1,9},{2,6},{3,11},{4,0},{5,13},{6,2},{7,15},{8,12},{9,1},{1... | collective-permute-start | bytes 663560 | tf_op jit(solution)/shard_map/ppermute | solution.py:71
  42.0 1.6 copy-start.4
  42.1 17.5 %collective-permute-start.2 = (bf16[96,2304]{1,0:T(8,128)(2,1)S(1)}, bf16[96,2304]{1,0:T(8,128)(2,1)S(1)}, u32[]{:S(2)}, u32[]{:S(2)}) collective-permute-start(bf16[96,2304]{1,0:T(8,128)(2,1)S(1)} %pad_maximum_fusion.1), channel_id=1, source_target_pairs={{0,16},{1,3},{2,18},{3,1},{4,20},{5,7},{6,22},{7,5},{8,24},{9,11},... | collective-permute-start | bytes 1327112 | tf_op jit(solution)/shard_map/ppermute | solution.py:71
  59.6 13.1 %collective-permute-start.3 = (bf16[192,2304]{1,0:T(8,128)(2,1)S(1)}, bf16[192,2304]{1,0:T(8,128)(2,1)S(1)}, u32[]{:S(2)}, u32[]{:S(2)}) collective-permute-start(bf16[192,2304]{1,0:T(8,128)(2,1)S(1)} %pad_maximum_fusion), channel_id=1, source_target_pairs={{0,2},{1,17},{2,0},{3,19},{4,6},{5,21},{6,4},{7,23},{8,10},{9,25},... | collective-permute-start | bytes 2654216 | tf_op jit(solution)/shard_map/ppermute | solution.py:71
  72.8 6.3 %copy-start = (bf16[384,2304]{1,0:T(8,128)(2,1)}, bf16[384,2304]{1,0:T(8,128)(2,1)S(1)}, u32[]{:S(2)}) copy-start(bf16[384,2304]{1,0:T(8,128)(2,1)S(1)} %constant_dynamic-update-slice_fusion) | copy-start | bytes 5308420
  72.8 6.3 %collective-permute-start.4 = (bf16[384,2304]{1,0:T(8,128)(2,1)S(1)}, bf16[384,2304]{1,0:T(8,128)(2,1)S(1)}, u32[]{:S(2)}, u32[]{:S(2)}) collective-permute-start(bf16[384,2304]{1,0:T(8,128)(2,1)S(1)} %constant_dynamic-update-slice_fusion), channel_id=1, source_target_pairs={{0,1},{1,0},{2,3},{3,2},{4,5},{5,4},{6,7},{7,6},{8,9},{9,8},{10,11... | collective-permute-start | bytes 5308424 | tf_op jit(solution)/shard_map/ppermute | solution.py:71
  79.0 1.2 copy-start.2
  162.1 9.2 %collective-permute-start.5 = (bf16[384,6912]{1,0:T(8,128)(2,1)}, bf16[384,6912]{1,0:T(8,128)(2,1)}, u32[]{:S(2)}, u32[]{:S(2)}) collective-permute-start(bf16[384,6912]{1,0:T(8,128)(2,1)} %get-tuple-element.87), channel_id=1, source_target_pairs={{0,1},{1,0},{2,3},{3,2},{4,5},{5,4},{6,7},{7,6},{8,9},{9,8},{10,11... | collective-permute-start | bytes 15925256 | tf_op jit(solution)/shard_map/ppermute | solution.py:71
  175.9 37.6 %collective-permute-start.7 = (bf16[192,6912]{1,0:T(8,128)(2,1)}, bf16[192,6912]{1,0:T(8,128)(2,1)S(1)}, u32[]{:S(2)}, u32[]{:S(2)}) collective-permute-start(bf16[192,6912]{1,0:T(8,128)(2,1)} %add_convert_fusion), channel_id=1, source_target_pairs={{0,2},{1,17},{2,0},{3,19},{4,6},{5,21},{6,4},{7,23},{8,10},{9,25},... | collective-permute-start | bytes 7962632 | tf_op jit(solution)/shard_map/ppermute | solution.py:71
  192.7 10.6 %collective-permute-start.6 = (bf16[384,2304]{1,0:T(8,128)(2,1)}, bf16[384,2304]{1,0:T(8,128)(2,1)}, u32[]{:S(2)}, u32[]{:S(2)}) collective-permute-start(bf16[384,2304]{1,0:T(8,128)(2,1)} %get-tuple-element.103), channel_id=1, source_target_pairs={{0,1},{1,0},{2,3},{3,2},{4,5},{5,4},{6,7},{7,6},{8,9},{9,8},{10,11... | collective-permute-start | bytes 5308424 | tf_op jit(solution)/shard_map/ppermute | solution.py:71
  205.9 23.9 %collective-permute-start.9 = (bf16[192,2304]{1,0:T(8,128)(2,1)}, bf16[192,2304]{1,0:T(8,128)(2,1)S(1)}, u32[]{:S(2)}, u32[]{:S(2)}) collective-permute-start(bf16[192,2304]{1,0:T(8,128)(2,1)} %add_convert_fusion.2), channel_id=1, source_target_pairs={{0,2},{1,17},{2,0},{3,19},{4,6},{5,21},{6,4},{7,23},{8,10},{9,25},... | collective-permute-start | bytes 2654216 | tf_op jit(solution)/shard_map/ppermute | solution.py:71
  216.8 18.1 %collective-permute-start.8 = (bf16[96,6912]{1,0:T(8,128)(2,1)}, bf16[96,6912]{1,0:T(8,128)(2,1)}, u32[]{:S(2)}, u32[]{:S(2)}) collective-permute-start(bf16[96,6912]{1,0:T(8,128)(2,1)} %add_convert_fusion.1), channel_id=1, source_target_pairs={{0,16},{1,3},{2,18},{3,1},{4,20},{5,7},{6,22},{7,5},{8,24},{9,11},... | collective-permute-start | bytes 3981320 | tf_op jit(solution)/shard_map/ppermute | solution.py:71
  229.8 7.8 %copy-start.3 = (bf16[192,2304]{1,0:T(8,128)(2,1)}, bf16[192,2304]{1,0:T(8,128)(2,1)S(1)}, u32[]{:S(2)}) copy-start(bf16[192,2304]{1,0:T(8,128)(2,1)S(1)} %collective-permute-done.9) | copy-start | bytes 2654212
  232.2 5.4 %copy-start.6 = (f32[16,768]{1,0:T(8,128)S(1)}, f32[16,768]{1,0:T(8,128)}, u32[]{:S(2)}) copy-start(f32[16,768]{1,0:T(8,128)} %table_grad.2) | copy-start | bytes 147460
  232.2 5.4 %copy-start.7 = (f32[16,768]{1,0:T(8,128)S(1)}, f32[16,768]{1,0:T(8,128)}, u32[]{:S(2)}) copy-start(f32[16,768]{1,0:T(8,128)} %table_grad.3) | copy-start | bytes 147460
  232.2 22.0 %collective-permute-start.10 = (bf16[96,2304]{1,0:T(8,128)(2,1)}, bf16[96,2304]{1,0:T(8,128)(2,1)}, u32[]{:S(2)}, u32[]{:S(2)}) collective-permute-start(bf16[96,2304]{1,0:T(8,128)(2,1)} %add_convert_fusion.4), channel_id=1, source_target_pairs={{0,16},{1,3},{2,18},{3,1},{4,20},{5,7},{6,22},{7,5},{8,24},{9,11},... | collective-permute-start | bytes 1327112 | tf_op jit(solution)/shard_map/ppermute | solution.py:71
  241.5 10.9 %all-to-all-start.1 = ((f32[32,1,624]{2,1,0:T(1,128)}), f32[32,1,624]{2,1,0:T(1,128)S(1)}, u32[]{:S(2)}, u32[]{:S(2)}) async-start(f32[32,1,624]{2,1,0:T(1,128)} %reshape.139), calls=%async_computation.1 | async-start | bytes 163840 | tf_op jit(solution)/shard_map/all_to_all | solution.py:1070
  244.6 18.2 %collective-permute-start.12 = (bf16[48,6912]{1,0:T(8,128)(2,1)}, bf16[48,6912]{1,0:T(8,128)(2,1)}, u32[]{:S(2)}, u32[]{:S(2)}) collective-permute-start(bf16[48,6912]{1,0:T(8,128)(2,1)} %add_convert_fusion.3), channel_id=1, source_target_pairs={{0,4},{1,9},{2,6},{3,11},{4,0},{5,13},{6,2},{7,15},{8,12},{9,1},{1... | collective-permute-start | bytes 1990664 | tf_op jit(solution)/shard_map/ppermute | solution.py:71
  255.6 11.9 %collective-permute-start.11 = (bf16[48,2304]{1,0:T(8,128)(2,1)S(1)}, bf16[48,2304]{1,0:T(8,128)(2,1)S(1)}, u32[]{:S(2)}, u32[]{:S(2)}) collective-permute-start(bf16[48,2304]{1,0:T(8,128)(2,1)S(1)} %add_convert_fusion.6), channel_id=1, source_target_pairs={{0,4},{1,9},{2,6},{3,11},{4,0},{5,13},{6,2},{7,15},{8,12},{9,1},{1... | collective-permute-start | bytes 663560 | tf_op jit(solution)/shard_map/ppermute | solution.py:71
  264.3 10.9 %collective-permute-start.14 = (bf16[24,6912]{1,0:T(8,128)(2,1)S(1)}, bf16[24,6912]{1,0:T(8,128)(2,1)S(1)}, u32[]{:S(2)}, u32[]{:S(2)}) collective-permute-start(bf16[24,6912]{1,0:T(8,128)(2,1)S(1)} %add_convert_fusion.5), channel_id=1, source_target_pairs={{0,8},{1,5},{2,10},{3,7},{4,12},{5,1},{6,14},{7,3},{8,0},{9,13},{1... | collective-permute-start | bytes 995336 | tf_op jit(solution)/shard_map/ppermute | solution.py:71
  268.6 12.7 %collective-permute-start.13 = (bf16[24,2304]{1,0:T(8,128)(2,1)S(1)}, bf16[24,2304]{1,0:T(8,128)(2,1)S(1)}, u32[]{:S(2)}, u32[]{:S(2)}) collective-permute-start(bf16[24,2304]{1,0:T(8,128)(2,1)S(1)} %add_convert_fusion.7), channel_id=1, source_target_pairs={{0,8},{1,5},{2,10},{3,7},{4,12},{5,1},{6,14},{7,3},{8,0},{9,13},{1... | collective-permute-start | bytes 331784 | tf_op jit(solution)/shard_map/ppermute | solution.py:71
Sparse Core Ops, SparseCore 0:
  11.5 97.9 all-gather.1
where the time goes:
time: 292 us; the launch traced here: 290 us
  Pallas kernels  146 us (50%)
  waiting for transfers between devices  53.2 us (18%)
  other arithmetic  32.1 us (11%)
  starting transfers between devices  26.4 us (9%)
  local copies, waits for them, and re-layouts  17.5 us (6%)
  between operations  14.3 us (5%)
    pallas_call x1, Pallas kernels, feed(): pl.pallas_call(functools.partial(feed_body, image, block_rows), grid=(ste...  52.7 us
    ppermute x15, waiting for transfers between devices, exchange(): lax.ppermute(values, AX, [(i, i ^ 1 << orders[i & 1][step]) for i in rang...  43.7 us
    convert_element_type x8, other arithmetic, scatter_step(): sum((piece[rows // 2:rows].astype(F32) for piece in pieces)).astype(BF16)  19.5 us
    ppermute x15, starting transfers between devices, exchange(): lax.ppermute(values, AX, [(i, i ^ 1 << orders[i & 1][step]) for i in rang...  19.4 us
    pallas_call x2, Pallas kernels, attend_back(): pl.pallas_call(functools.partial(attend_back_body, block_rows, head_dim *...  16.7 us
    pallas_call x2, Pallas kernels, table_grad(): pl.pallas_call(functools.partial(table_grad_body, heads, groups), grid=(1...  14.6 us
    pallas_call x1, Pallas kernels, attend(): pl.pallas_call(functools.partial(attend_body, block_rows), grid=(pairs,),...  11.6 us
    pallas_call x1, Pallas kernels, input_grad(): pl.pallas_call(functools.partial(input_grad_body, image, block_rows), gri...  10.6 us
  transfers between devices with their start and end apart: 18, of which 11 were waited for; matrix products, arithmetic and copies ran while one was open for 14% of the time, Pallas kernels for 32%

commit v1 on v0

--- a/solution.py
+++ b/solution.py
@@ -59,20 +59,24 @@
     return pl.BlockSpec(memory_space=pltpu.SMEM)
 
 
-def exchange_orders(count):
+def exchange_orders(count, kind):
     bits = count.bit_length() - 1
     if bits < 3:
         return (list(range(bits)),) * 2
     rest = list(range(2, bits - 1))
-    return [0, 1, bits - 1] + rest, [0, bits - 1, 1] + rest[::-1]
-
-def exchange(values, step, count):
-    orders = exchange_orders(count)
+    outer = [1, bits - 1]
+    if kind == 0:
+        return [0] + outer + rest, [0] + outer[::-1] + rest[::-1]
+    return [0] + rest + outer, [0] + rest[::-1] + outer[::-1]
+
+
+def exchange(values, step, count, kind):
+    orders = exchange_orders(count, kind)
     return lax.ppermute(values, AX, [(i, i ^ (1 << orders[i & 1][step])) for i in range(count)])
 
 
-def exchange_owners(count):
-    orders = exchange_orders(count)
+def exchange_owners(count, kind):
+    orders = exchange_orders(count, kind)
     bits = len(orders[0])
     me = lax.axis_index(AX)
     spot = jnp.arange(count, dtype=jnp.int32)
@@ -89,7 +93,7 @@
 
 def gather_halves(values, count, before):
     for number, step in enumerate(reversed(range(count.bit_length() - 1))):
-        got = exchange(values, step, count)
+        got = exchange(values, step, count, 0)
         if number < len(before):
             got = after(got, *before[number])
         if step == 0:
@@ -99,14 +103,17 @@
     return values[:half], values[half:]
 
 
-def scatter_step(pieces, send, step, count, *others):
-    got = after(exchange(send, step, count), *others)
+def scatter_step(kind, pieces, send, step, count, *others):
+    got = after(exchange(send, step, count, kind), *others)
     pieces = pieces + [got]
-    rows = got.shape[0]
+    rows = got.shape[-2]
+
+    def total(start, stop):
+        return sum(piece[..., start:stop, :].astype(F32) for piece in pieces)
+
     if step == count.bit_length() - 2:
-        return sum(piece[:rows].astype(F32) for piece in pieces), None
-    send = sum(piece[rows // 2 : rows].astype(F32) for piece in pieces).astype(BF16)
-    return pieces, send
+        return total(0, rows), None
+    return pieces, total(rows // 2, rows).astype(BF16)
 
 
 def in_chunks(rows, size, body):
@@ -380,25 +387,25 @@
     )(owners, normed, vec, mine.reshape(half, own, wide), got.reshape(half, own, wide))
 
 
-def turn_body(order_ref, vec_ref, cb_ref, low_ref, up_ref, up_t_ref, low_t_ref):
-    up = (vec_ref[GAM_M : GAM_M + 1, :] * cb_ref[...].astype(F32)).astype(BF16)
-    up_ref[...] = up
+def turn_body(order_ref, qkv_order_ref, vec_ref, cb_ref, low_ref, up_ref, up_t_ref, low_t_ref):
+    up_ref[...] = (vec_ref[GAM_M : GAM_M + 1, :] * cb_ref[...].astype(F32)).astype(BF16)
     width = low_ref.shape[1]
 
     def turned(here):
-        order = row_order(order_ref[here, :], width)
-        up_t_ref[here, :] = nt(order, up_ref[...]).astype(BF16)
-        low_t_ref[here, :] = nt(order, low_ref[...]).astype(BF16)
+        up_t_ref[here, :] = nt(row_order(order_ref[here, :], width), up_ref[...]).astype(BF16)
+        qkv_order = row_order(qkv_order_ref[here, :], width)
+        low_t_ref[here, :] = nt(qkv_order, low_ref[...]).astype(BF16)
 
     in_chunks(width, width // 2, turned)
 
 
-def turn(order, vec, cb, low):
+def turn(order, qkv_order, vec, cb, low):
     rows, width = cb.shape
     return pl.pallas_call(
         turn_body,
         grid=(1,),
-        in_specs=[full((width, 1)), full(vec.shape), full((rows, width)), full((rows, width))],
+        in_specs=[full((width, 1))] * 2
+        + [full(vec.shape), full((rows, width)), full((rows, width))],
         out_specs=[full((rows, width)), full((width, rows)), full((width, rows))],
         out_shape=[
             jax.ShapeDtypeStruct((rows, width), BF16),
@@ -408,7 +415,7 @@
         compiler_params=params(),
         cost_estimate=cost(3),
         name="turn",
-    )(order, vec, cb, low)
+    )(order, qkv_order, vec, cb, low)
 
 
 def halves(values):
@@ -606,16 +613,15 @@
     rows, width = xb_ref.shape
     late = Late((cb_any,), (cb_s,), sems)
 
-    half = keep_ref.shape[0]
-
-    def put_grads(columns, turned_ref, values):
-        def one(here):
-            size = here.size
-            keep_ref[here, columns] = nn(turned_ref[here, :], values).astype(BF16)
-            there = pl.ds(pl.multiple_of(half + here.start, 16), size)
-            send_ref[here, columns] = nn(turned_ref[there, :], values).astype(BF16)
-
-        in_chunks(half, half // 2, one)
+    half = keep_ref.shape[1]
+    side = width // 2
+
+    def put_out_grad(here):
+        there = pl.ds(pl.multiple_of(half + here.start, 16), here.size)
+        for ref, rows_here in ((keep_ref, here), (send_ref, there)):
+            values = nn(turned_s[rows_here, :], mixed_ref[...]).astype(BF16)
+            ref[0, here, :side] = values[:, :side]
+            ref[1, here, :side] = values[:, side:]
 
     def turn_low():
         def turned(here):
@@ -645,7 +651,6 @@
 
     @pl.when(step < last)
     def _():
-        tile = fc1_ref.shape[1]
         pre = nn(low_s[...], fc1_ref[...]) + bias_ref[0:1, :]
         phi, density = cumulative(pre)
         hidden = (pre * phi).astype(BF16)
@@ -653,12 +658,9 @@
         grad = (nn(up_ref[...], fc2_ref[...]) * slope).astype(BF16)
         ff_s[...] += nt(hidden, fc2_ref[...])
         second_s[...] += nt(grad, fc1_ref[...])
-        for columns, values in (
-            (slice(0, tile), nn(turned_s[...], grad)),
-            (slice(tile, 2 * tile), nn(up_t_ref[...], hidden)),
-        ):
-            keep_ref[:, columns] = values[:half].astype(BF16)
-            send_ref[:, columns] = values[half:].astype(BF16)
+        for plane, values in enumerate((nn(turned_s[...], grad), nn(up_t_ref[...], hidden))):
+            keep_ref[plane] = values[:half].astype(BF16)
+            send_ref[plane] = values[half:].astype(BF16)
         fc1_sum_ref[...] = jnp.broadcast_to(
             jnp.sum(grad.astype(F32), axis=0, keepdims=True), fc1_sum_ref.shape
         )
@@ -683,7 +685,7 @@
         mixed_grad_ref[...] = nn(low, out_w_ref[...]).astype(BF16)
         low_s[...] = low
         turn_low()
-        put_grads(slice(0, width), turned_s, mixed_ref[...])
+        in_chunks(half, half // 2, put_out_grad)
         branch = ff_s[...] + vec_ref[FC2_B : FC2_B + 1, :]
         result = (after_s[...] + vec_ref[GAM_M : GAM_M + 1, :] * branch).astype(BF16)
         out_ref[...] = restore_rows(info[0], result, block_rows, image, out_ref.shape[0]).astype(
@@ -740,8 +742,8 @@
         + [anywhere],
         out_specs=[
             full((length, width)),
-            pl.BlockSpec((width // 2, 2 * tile), lambda i: (0, i)),
-            pl.BlockSpec((width // 2, 2 * tile), lambda i: (0, i)),
+            pl.BlockSpec((2, width // 2, tile), lambda i: (0, 0, i)),
+            pl.BlockSpec((2, width // 2, tile), lambda i: (0, 0, i)),
             pl.BlockSpec((8, tile), lambda i: (0, at(i))),
             full((rows, width)),
             full((rows, width)),
@@ -749,8 +751,8 @@
         ],
         out_shape=[
             jax.ShapeDtypeStruct((length, width), BF16),
-            jax.ShapeDtypeStruct((width // 2, 2 * hidden + width), BF16),
-            jax.ShapeDtypeStruct((width // 2, 2 * hidden + width), BF16),
+            jax.ShapeDtypeStruct((2, width // 2, hidden + width // 2), BF16),
+            jax.ShapeDtypeStruct((2, width // 2, hidden + width // 2), BF16),
             jax.ShapeDtypeStruct((8, hidden), F32),
             jax.ShapeDtypeStruct((rows, width), BF16),
             jax.ShapeDtypeStruct((rows, width), F32),
@@ -1003,8 +1005,12 @@
         fc2_bias[None],
         gamma_mlp[None],
     ]
-    owners = exchange_owners(count)
-    order = (owners[:, None] * own + jnp.arange(own, dtype=jnp.int32)).reshape(-1, 1)
+    owners = exchange_owners(count, 0)
+
+    def row_places(owning):
+        return (owning[:, None] * own + jnp.arange(own, dtype=jnp.int32)).reshape(-1, 1)
+
+    order, qkv_order = row_places(owners), row_places(exchange_owners(count, 1))
     later = lax.all_gather(
         jnp.concatenate([fc1_weight, fc2_weight.T, out_weight.T], axis=1), AX, axis=0, tiled=True
     )
@@ -1017,7 +1023,7 @@
     packed, low, qkv_full = project(owners, normed, vec, mine, got, head_dim)
     qkv_full = qkv_full.reshape(width, -1)
     mixed, weights = attend(info, packed, table, block_rows)
-    up, up_t, low_t = turn(order, vec, after(cb, mixed), low)
+    up, up_t, low_t = turn(order, qkv_order, vec, after(cb, mixed), low)
     tile = 512
     out, feed_keep, feed_send, fc1_sum, mixed_grad, after_grad, sums2 = feed(
         info,
@@ -1037,18 +1043,20 @@
     )
     pairs = heads // 2
     some = attend_back(packed, weights, mixed_grad, head_dim, 256, 0, pairs // 2)
-    a_pieces, a_send = scatter_step([feed_keep], feed_send, 0, count, some[0])
+    a_pieces, a_send = scatter_step(0, [feed_keep], feed_send, 0, count, some[0])
     packed_grad, table_sum = attend_back(
         packed, weights, after(mixed_grad, a_send), head_dim, 256, pairs // 2, pairs, some
     )
     qkv_keep, qkv_send = weight_grad(low_t, packed_grad)
+    biases = after(fc1_sum, qkv_keep)[0].reshape(count, -1, own)
+    b_pieces, b_send = scatter_step(1, [qkv_keep], qkv_send, 0, count, biases)
     in_grad, sums1 = input_grad(
         info,
         packed_grad,
         qkv_full,
         vec,
         normed,
-        after(inv, qkv_keep),
+        after(inv, b_send),
         after_grad,
         image,
         block_rows,
@@ -1056,29 +1064,30 @@
     )
     groups = -(-image // 8)
     slots = own * count
-    b_pieces, b_send = scatter_step([qkv_keep], qkv_send, 0, count, in_grad)
-    slot_sums = table_grad(after(table_sum, b_send), moved, slots, (0, groups // 2))
-    a_pieces, a_send = scatter_step(a_pieces, a_send, 1, count, slot_sums)
-    more_sums = table_grad(after(table_sum, a_send), moved, slots, (groups // 2, groups))
-    b_pieces, b_send = scatter_step(b_pieces, b_send, 1, count, more_sums)
-    a_pieces, a_send = scatter_step(a_pieces, a_send, 2, count, b_send)
-    slot_sums = slot_sums + after(more_sums, a_send)
+    a_pieces, a_send = scatter_step(0, a_pieces, a_send, 1, count, in_grad)
+    slot_sums = table_grad(after(table_sum, a_send), moved, slots, (0, groups // 2))
+    b_pieces, b_send = scatter_step(1, b_pieces, b_send, 1, count, slot_sums)
+    more_sums = table_grad(after(table_sum, b_send), moved, slots, (groups // 2, groups))
+    a_pieces, a_send = scatter_step(0, a_pieces, a_send, 2, count, more_sums)
+    b_pieces, b_send = scatter_step(1, b_pieces, b_send, 2, count, a_send)
+    slot_sums = slot_sums + after(more_sums, b_send)
 
     rows = jnp.concatenate([sums1[:10] + sums2[:10], slot_sums[:heads]], axis=0)
     rows = jnp.transpose(rows.reshape(-1, count, own), (1, 0, 2))
-    biases = fc1_sum[0].reshape(count, -1, own)
     swapped = lax.all_to_all(jnp.concatenate([rows, biases], axis=1), AX, 0, 0, tiled=True)
-    b_pieces, b_send = scatter_step(b_pieces, b_send, 2, count, swapped)
-    for step in range(3, count.bit_length() - 1):
-        a_pieces, a_send = scatter_step(a_pieces, a_send, step, count, b_pieces)
-        b_pieces, b_send = scatter_step(b_pieces, b_send, step, count, a_pieces)
+    a_pieces, a_send = scatter_step(0, a_pieces, a_send, 3, count, swapped)
+    b_pieces, b_send = scatter_step(1, b_pieces, b_send, 3, count, a_send)
+    late_send = b_send
+    for step in range(4, count.bit_length() - 1):
+        a_pieces, a_send = scatter_step(0, a_pieces, a_send, step, count, b_send)
+    for step in range(4, count.bit_length() - 1):
+        b_pieces, b_send = scatter_step(1, b_pieces, b_send, step, count, a_pieces)
     feed_wide, qkv_shard = a_pieces, b_pieces
-    small_shard = jnp.sum(swapped, axis=0)
-
-    pieces = feed_wide[:, : 2 * hidden].reshape(own, hidden // tile, 2, tile)
-    grad_fc1 = pieces[:, :, 0].reshape(own, hidden)
-    grad_fc2 = pieces[:, :, 1].reshape(own, hidden).T
-    grad_out = feed_wide[:, 2 * hidden :].T
+    small_shard = jnp.sum(after(swapped, late_send), axis=0)
+
+    grad_fc1 = feed_wide[0, :, :hidden]
+    grad_fc2 = feed_wide[1, :, :hidden].T
+    grad_out = jnp.concatenate([feed_wide[0, :, hidden:], feed_wide[1, :, hidden:]], axis=1).T
     grad_table = small_shard[10 : 10 + heads, :per_device]
     grad_fc1_bias = small_shard[10 + heads :].reshape(-1)
     return (

time: 292 us -> 285 us (0.976)
  local copies, waits for them, and re-layouts: 17.5 us -> 13 us
    ppermute x15, waiting for transfers between devices: 43.7 us -> 36.6 us  [exchange(): lax.ppermute(values, AX, [(i, i ^ 1 << orders[i & 1][step]) for i in rang...]
    all_gather x1, waiting for transfers between devices: 2.09 us -> 6.34 us  [local(): lax.all_gather(jnp.concatenate([fc1_weight, fc2_weight.T, out_weight.T],...]
  transfers between devices with their start and end apart: 18 -> 18, of which waited for: 11 -> 11; matrix products, arithmetic and copies ran while one was open for 14% -> 13% of each run, Pallas kernels for 32% -> 33%
where the time goes in v1:
time: 285 us; the launch traced here: 283 us
  Pallas kernels  147 us (52%)
  waiting for transfers between devices  52.3 us (18%)
  other arithmetic  32.8 us (12%)
  starting transfers between devices  24.1 us (8%)
  between operations  14.3 us (5%)
  local copies, waits for them, and re-layouts  13 us (5%)
    pallas_call x1, Pallas kernels, feed(): pl.pallas_call(functools.partial(feed_body, image, block_rows), grid=(ste...  52.6 us
    ppermute x15, waiting for transfers between devices, exchange(): lax.ppermute(values, AX, [(i, i ^ 1 << orders[i & 1][step]) for i in rang...  36.6 us
    convert_element_type x8, other arithmetic, scatter_step(): return (pieces, total(rows // 2, rows).astype(BF16))  20.9 us
    ppermute x15, starting transfers between devices, exchange(): lax.ppermute(values, AX, [(i, i ^ 1 << orders[i & 1][step]) for i in rang...  17 us
    pallas_call x2, Pallas kernels, attend_back(): pl.pallas_call(functools.partial(attend_back_body, block_rows, head_dim *...  16.7 us
    pallas_call x2, Pallas kernels, table_grad(): pl.pallas_call(functools.partial(table_grad_body, heads, groups), grid=(1...  14.9 us
    pallas_call x1, Pallas kernels, attend(): pl.pallas_call(functools.partial(attend_body, block_rows), grid=(pairs,),...  11.6 us
    pallas_call x1, Pallas kernels, input_grad(): pl.pallas_call(functools.partial(input_grad_body, image, block_rows), gri...  10.6 us
  transfers between devices with their start and end apart: 18, of which 11 were waited for; matrix products, arithmetic and copies ran while one was open for 13% of the time, Pallas kernels for 33%

profile of v1, /device:TPU:0, one launch (start us, length us, event | category | flops | bytes accessed | tf_op | source)
XLA Modules:
  0.0 283.4 jit_solution(10782754218625319182)
XLA Ops:
  7.2 1.8 pad_maximum_fusion.3
  9.0 4.1 %collective-permute-start = (bf16[24,2304]{1,0:T(8,128)(2,1)}, bf16[24,2304]{1,0:T(8,128)(2,1)S(1)}, u32[]{:S(2)}, u32[]{:S(2)}) collective-permute-start(bf16[24,2304]{1,0:T(8,128)(2,1)} %param.26), channel_id=1, source_target_pairs={{0,8},{1,5},{2,10},{3,7},{4,12},{5,1},{6,14},{7,3},{8,0},{9,13},{1... | collective-permute-start | bytes 331784 | tf_op jit(solution)/shard_map/ppermute | solution.py:75
  13.1 1.6 pack.1
  14.7 0.7 compare_reduce_fusion
  15.4 0.6 select_reduce_fusion.1
  16.0 1.9 pad_add_fusion.info
  17.9 7.4 %prepare.1 = (bf16[832,768]{1,0:T(8,128)(2,1)}, bf16[832,768]{1,0:T(8,128)(2,1)}, f32[832,768]{1,0:T(8,128)}, f32[832,128]{1,0:T(8,128)}) custom-call(s32[2]{0:T(128)} %pad_add_fusion.info, bf16[788,768]{1,0:T(8,128)(2,1)} %bitcast.42, bf16[788,768]{1,0:T(8,128)(2,1)} %bitcast.43), custom_call_target="tpu_custom_call" | custom-call | flops 80000000 | bytes 80000 | tf_op jit(solution)/shard_map/prepare/pallas_call | solution.py:220
  25.3 0.7 broadcast_in_dim.82
  26.0 3.8 %all-to-all-start = ((bf16[32,24,128]{2,1,0:T(8,128)(2,1)}), bf16[32,24,128]{2,1,0:T(8,128)(2,1)S(1)}, u32[]{:S(2)}, u32[]{:S(2)}) async-start(bf16[32,24,128]{2,1,0:T(8,128)(2,1)} %broadcast_in_dim.82), calls=%async_computation | async-start | bytes 393216 | tf_op jit(solution)/shard_map/all_to_all | solution.py:1020
  29.9 1.8 collective-permute-start.1
  31.7 8.6 %collective-permute-done.1 = bf16[48,2304]{1,0:T(8,128)(2,1)S(1)} collective-permute-done((bf16[48,2304]{1,0:T(8,128)(2,1)S(1)}, bf16[48,2304]{1,0:T(8,128)(2,1)S(1)}, u32[]{:S(2)}, u32[]{:S(2)}) %collective-permute-start.1) | collective-permute-done | bytes 221216 | tf_op jit(solution)/shard_map/ppermute | solution.py:75
  40.4 1.0 all-to-all-done
  41.4 0.7 collective-permute-start.2
  42.3 0.7 pad.4.index_ref
  43.0 9.1 %expand.1 = (f32[64,768]{1,0:T(8,128)}, f32[8,3072]{1,0:T(8,128)}, f32[12,208,256]{2,1,0:T(8,128)}) custom-call(bf16[768,128]{1,0:T(8,128)(2,1)} %bitcast.44, s32[208,256]{1,0:T(8,128)} %pad.4.index_ref), custom_call_target="tpu_custom_call" | custom-call | flops 100000000 | bytes 80000 | tf_op jit(solution)/shard_map/expand/pallas_call | solution.py:289
  52.1 5.5 %collective-permute-done.2 = bf16[96,2304]{1,0:T(8,128)(2,1)S(1)} collective-permute-done((bf16[96,2304]{1,0:T(8,128)(2,1)S(1)}, bf16[96,2304]{1,0:T(8,128)(2,1)S(1)}, u32[]{:S(2)}, u32[]{:S(2)}) %collective-permute-start.2) | collective-permute-done | bytes 442400 | tf_op jit(solution)/shard_map/ppermute | solution.py:75
  57.9 12.9 %collective-permute-done.3 = bf16[192,2304]{1,0:T(8,128)(2,1)S(1)} collective-permute-done((bf16[192,2304]{1,0:T(8,128)(2,1)S(1)}, bf16[192,2304]{1,0:T(8,128)(2,1)S(1)}, u32[]{:S(2)}, u32[]{:S(2)}) %collective-permute-start.3) | collective-permute-done | bytes 884768 | tf_op jit(solution)/shard_map/ppermute | solution.py:75
  71.0 0.6 broadcast_multiply_fusion
  71.7 0.9 add.201.order_ref
  72.7 0.9 add.202.qkv_order_ref
  73.6 1.0 collective-permute-done.4
  74.6 1.2 copy-done.2
  75.9 9.2 %project.1 = (bf16[832,2304]{1,0:T(8,128)(2,1)}, bf16[832,768]{1,0:T(8,128)(2,1)}, bf16[32,24,2304]{2,1,0:T(8,128)(2,1)}) custom-call(s32[32]{0:T(128)} %get-tuple-element.166.owners, f32[832,768]{1,0:T(8,128)} %get-tuple-element.69.normed_ref.normed_any, f32[64,768]{1,0:T(8,128)} %get-tuple-element.72.vec_ref, bf16[16,24,2304]{2,1,0:T(8,128)(2,1)} %bitcast.37, ...), custom_call_target="tpu_custom_call" | custom-call | flops 80000000 | bytes 80000 | tf_op jit(solution)/shard_map/project/pallas_call | solution.py:365
  85.1 11.6 %attend.1 = (bf16[832,768]{1,0:T(8,128)(2,1)}, f32[12,4,208,208]{3,2,1,0:T(8,128)}) custom-call(s32[2]{0:T(128)} %pad_add_fusion.info, bf16[832,2304]{1,0:T(8,128)(2,1)} %get-tuple-element.77.q_ref.k_ref.v_ref, bf16[832,2304]{1,0:T(8,128)(2,1)} %get-tuple-element.77.q_ref.k_ref.v_ref, bf16[832,2304]{1,0:T(8,128)(2,1)} %get-tuple-element.77.q_ref.k_ref.v_ref, ...), custom_call_target="tpu_custom_call" | custom-call | flops 120000000 | bytes 80000 | tf_op jit(solution)/shard_map/attend/pallas_call | solution.py:458
  96.7 6.3 %turn.1 = (bf16[832,768]{1,0:T(8,128)(2,1)}, bf16[768,832]{1,0:T(8,128)(2,1)}, bf16[768,832]{1,0:T(8,128)(2,1)}) custom-call(s32[768,1]{1,0:T(8,128)} %add.201.order_ref, s32[768,1]{1,0:T(8,128)} %add.202.qkv_order_ref, f32[64,768]{1,0:T(8,128)} %get-tuple-element.72.vec_ref, bf16[832,768]{1,0:T(8,128)(2,1)} %get-tuple-element.80.cb_ref.cb_any, ...), custom_call_target="tpu_custom_call" | custom-call | flops 60000000 | bytes 80000 | tf_op jit(solution)/shard_map/turn/pallas_call | solution.py:404
  103.0 6.3 %all-gather.2.cloned.1.call-done.out_w_ref.fc1_ref.fc2_ref = bf16[768,6912]{1,0:T(8,128)(2,1)} async-done(((bf16[24,6912]{1,0:T(8,128)(2,1)}), bf16[768,6912]{1,0:T(8,128)(2,1)}) %all-gather.2.cloned.1.call-update) | async-done | bytes 10616848 | tf_op jit(solution)/shard_map/all_gather | solution.py:1014
  109.3 52.6 %feed.1 = (bf16[788,768]{1,0:T(8,128)(2,1)}, bf16[2,384,3456]{2,1,0:T(8,128)(2,1)}, bf16[2,384,3456]{2,1,0:T(8,128)(2,1)}, f32[8,3072]{1,0:T(8,128)}, bf16[832,7...) custom-call(s32[2]{0:T(128)} %pad_add_fusion.info, s32[768,1]{1,0:T(8,128)} %add.201.order_ref, ...), custom_call_target="tpu_custom_call" | custom-call | flops 560000000 | bytes 80000 | tf_op jit(solution)/shard_map/feed/pallas_call | solution.py:726
  162.2 8.3 %attend_back.2 = (bf16[3,832,768]{2,1,0:T(8,128)(2,1)}, f32[12,208,256]{2,1,0:T(8,128)}) custom-call(bf16[832,2304]{1,0:T(8,128)(2,1)} %get-tuple-element.77.q_ref.k_ref.v_ref, bf16[832,2304]{1,0:T(8,128)(2,1)} %get-tuple-element.77.q_ref.k_ref.v_ref, bf16[832,2304]{1,0:T(8,128)(2,1)} %get-tuple-element.77.q_ref.k_ref.v_ref, ...), custom_call_target="tpu_custom_call" | custom-call | flops 80000000 | bytes 80000 | tf_op jit(solution)/shard_map/attend_back/pallas_call | solution.py:516
  171.0 4.6 %add_convert_fusion = bf16[2,192,3456]{2,1,0:T(8,128)(2,1)} fusion(bf16[2,384,3456]{2,1,0:T(8,128)(2,1)} %collective-permute-done.5, bf16[2,384,3456]{2,1,0:T(8,128)(2,1)} %get-tuple-element.88), kind=kLoop, calls=%fused_computation | loop fusion | flops 5308416 | bytes 7962624 | tf_op jit(solution)/shard_map/convert_element_type | solution.py:116
  175.7 1.5 collective-permute-start.7
  177.2 8.3 %attend_back.3 = (bf16[3,832,768]{2,1,0:T(8,128)(2,1)}, f32[12,208,256]{2,1,0:T(8,128)}) custom-call(bf16[832,2304]{1,0:T(8,128)(2,1)} %get-tuple-element.77.q_ref.k_ref.v_ref, bf16[832,2304]{1,0:T(8,128)(2,1)} %get-tuple-element.77.q_ref.k_ref.v_ref, ...), custom_call_target="tpu_custom_call", output_to_operand_aliasing={{0}: (5, {}), {1}: (6, {})} | custom-call | flops 80000000 | bytes 80000 | tf_op jit(solution)/shard_map/attend_back/pallas_call | solution.py:516
  185.5 6.9 %weight_grad.1 = (bf16[384,2304]{1,0:T(8,128)(2,1)}, bf16[384,2304]{1,0:T(8,128)(2,1)}) custom-call(bf16[768,832]{1,0:T(8,128)(2,1)} %get-tuple-element.97.low_t_ref, bf16[3,832,768]{2,1,0:T(8,128)(2,1)} %get-tuple-element.94.packed_ref), custom_call_target="tpu_custom_call" | custom-call | flops 100000000 | bytes 80000 | tf_op jit(solution)/shard_map/weight_grad/pallas_call | solution.py:798
  192.4 0.9 slice_reduce_fusion.8
  193.3 0.8 reshape_squeeze.3
  194.1 2.4 collective-permute-done.6
  196.4 2.6 add_convert_fusion.2
  199.0 1.3 collective-permute-start.8
  200.3 10.6 %input_grad.1 = (bf16[788,768]{1,0:T(8,128)(2,1)}, f32[16,768]{1,0:T(8,128)}) custom-call(s32[2]{0:T(128)} %pad_add_fusion.info, bf16[3,832,768]{2,1,0:T(8,128)(2,1)} %get-tuple-element.94.packed_ref, bf16[768,2304]{1,0:T(8,128)(2,1)} %bitcast.36, f32[64,768]{1,0:T(8,128)} %get-tuple-element.72.vec_ref, f32[832,768]{1,0:T(8,128)} %get-tuple-element.69.normed_ref.normed_any, ...), custom_call_target="tpu_custom_call" | custom-call | flops 160000000 | bytes 80000 | tf_op jit(solution)/shard_map/input_grad/pallas_call | solution.py:864
  210.9 3.3 %add_convert_fusion.1 = bf16[2,96,3456]{2,1,0:T(8,128)(2,1)} fusion(bf16[2,192,3456]{2,1,0:T(8,128)(2,1)S(1)} %collective-permute-done.7, bf16[2,384,3456]{2,1,0:T(8,128)(2,1)} %collective-permute-done.5, bf16[2,384,3456]{2,1,0:T(8,128)(2,1)} %get-tuple-element.88), kind=kLoop, calls=%fused_computation.1 | loop fusion | flops 3981312 | bytes 5308416 | tf_op jit(solution)/shard_map/convert_element_type | solution.py:116
  215.4 7.1 %table_grad.2 = f32[16,768]{1,0:T(8,128)} custom-call(f32[12,208,256]{2,1,0:T(8,128)} %get-tuple-element.112.table_ref, s32[208,256]{1,0:T(8,128)} %pad.4.index_ref), custom_call_target="tpu_custom_call" | custom-call | flops 160000000 | bytes 80000 | tf_op jit(solution)/shard_map/table_grad/pallas_call | solution.py:947
  222.5 1.6 add_convert_fusion.4
  224.2 1.1 collective-permute-start.9
  225.3 7.8 %table_grad.3 = f32[16,768]{1,0:T(8,128)} custom-call(f32[12,208,256]{2,1,0:T(8,128)} %get-tuple-element.112.table_ref, s32[208,256]{1,0:T(8,128)} %pad.4.index_ref), custom_call_target="tpu_custom_call" | custom-call | flops 160000000 | bytes 80000 | tf_op jit(solution)/shard_map/table_grad/pallas_call | solution.py:947
  233.1 2.7 add_convert_fusion.3
  235.8 1.6 collective-permute-start.12
  237.4 0.9 collective-permute-done.9
  238.3 1.9 add_convert_fusion.6
  240.5 0.9 pad_maximum_fusion.2
  241.7 0.9 reshape.169
  242.6 3.2 %all-to-all-start.1 = ((f32[32,1,624]{2,1,0:T(1,128)}), f32[32,1,624]{2,1,0:T(1,128)S(1)}, u32[]{:S(2)}, u32[]{:S(2)}) async-start(f32[32,1,624]{2,1,0:T(1,128)} %reshape.169), calls=%async_computation.1 | async-start | bytes 163840 | tf_op jit(solution)/shard_map/all_to_all | solution.py:1077
  245.9 1.8 collective-permute-start.11
  247.7 8.3 %all-to-all-done.1 = f32[32,1,624]{2,1,0:T(1,128)S(1)} async-done(((f32[32,1,624]{2,1,0:T(1,128)}), f32[32,1,624]{2,1,0:T(1,128)S(1)}, u32[]{:S(2)}, u32[]{:S(2)}) %all-to-all-start.1) | async-done | bytes 79904 | tf_op jit(solution)/shard_map/all_to_all | solution.py:1077
  256.5 0.8 reduce.22
  257.6 2.3 add_convert_fusion.5
  259.9 0.6 collective-permute-start.14
  260.5 1.8 add_convert_fusion.7
  262.3 1.5 collective-permute-start.13
  264.0 0.7 copy.63
  266.0 0.8 slice_reduce_fusion
  266.9 4.8 %collective-permute-done.14 = bf16[2,24,3456]{2,1,0:T(8,128)(2,1)S(1)} collective-permute-done((bf16[2,24,3456]{2,1,0:T(8,128)(2,1)}, bf16[2,24,3456]{2,1,0:T(8,128)(2,1)S(1)}, u32[]{:S(2)}, u32[]{:S(2)}) %collective-permute-start.14) | collective-permute-done | bytes 331808 | tf_op jit(solution)/shard_map/ppermute | solution.py:75
  271.6 1.5 convert_add_fusion
  273.2 0.9 slice_bitcast_fusion
  274.0 1.9 convert_add_fusion.1
  275.9 0.6 maximum_bitcast_fusion
  (66 shorter events, 5.8 us)
Async XLA Ops:
  7.2 102.1 %all-gather.2.cloned.1.call-start = ((), (), s32[]{:S(2)}) async-start(), calls=%async_computation.2 | async-start | bytes 10948608 | tf_op jit(solution)/shard_map/all_gather | solution.py:1014
  9.0 20.9 %copy-start.1 = (bf16[24,2304]{1,0:T(8,128)(2,1)S(1)}, bf16[24,2304]{1,0:T(8,128)(2,1)}, u32[]{:S(2)}) copy-start(bf16[24,2304]{1,0:T(8,128)(2,1)} %param.26) | copy-start | bytes 331780
  9.0 20.8 %collective-permute-start = (bf16[24,2304]{1,0:T(8,128)(2,1)}, bf16[24,2304]{1,0:T(8,128)(2,1)S(1)}, u32[]{:S(2)}, u32[]{:S(2)}) collective-permute-start(bf16[24,2304]{1,0:T(8,128)(2,1)} %param.26), channel_id=1, source_target_pairs={{0,8},{1,5},{2,10},{3,7},{4,12},{5,1},{6,14},{7,3},{8,0},{9,13},{1... | collective-permute-start | bytes 331784 | tf_op jit(solution)/shard_map/ppermute | solution.py:75
  14.7 10.6 %copy-start.11 = (bf16[24,128]{1,0:T(8,128)(2,1)S(1)}, bf16[24,128]{1,0:T(8,128)(2,1)}, u32[]{:S(2)}) copy-start(bf16[24,128]{1,0:T(8,128)(2,1)} %pack.1) | copy-start | bytes 18436
  17.9 24.2 %copy-start.6 = (s32[197,197]{1,0:T(8,128)S(1)}, s32[197,197]{1,0:T(8,128)}, u32[]{:S(2)}) copy-start(s32[197,197]{1,0:T(8,128)} %param.23) | copy-start | bytes 465712
  26.0 15.4 %all-to-all-start = ((bf16[32,24,128]{2,1,0:T(8,128)(2,1)}), bf16[32,24,128]{2,1,0:T(8,128)(2,1)S(1)}, u32[]{:S(2)}, u32[]{:S(2)}) async-start(bf16[32,24,128]{2,1,0:T(8,128)(2,1)} %broadcast_in_dim.82), calls=%async_computation | async-start | bytes 393216 | tf_op jit(solution)/shard_map/all_to_all | solution.py:1020
  29.9 10.5 %collective-permute-start.1 = (bf16[48,2304]{1,0:T(8,128)(2,1)S(1)}, bf16[48,2304]{1,0:T(8,128)(2,1)S(1)}, u32[]{:S(2)}, u32[]{:S(2)}) collective-permute-start(bf16[48,2304]{1,0:T(8,128)(2,1)S(1)} %pad_maximum_fusion.4), channel_id=1, source_target_pairs={{0,4},{1,9},{2,6},{3,11},{4,0},{5,13},{6,2},{7,15},{8,12},{9,1},{1... | collective-permute-start | bytes 663560 | tf_op jit(solution)/shard_map/ppermute | solution.py:75
  41.4 1.6 copy-start.4
  41.4 16.2 %collective-permute-start.2 = (bf16[96,2304]{1,0:T(8,128)(2,1)S(1)}, bf16[96,2304]{1,0:T(8,128)(2,1)S(1)}, u32[]{:S(2)}, u32[]{:S(2)}) collective-permute-start(bf16[96,2304]{1,0:T(8,128)(2,1)S(1)} %pad_maximum_fusion.1), channel_id=1, source_target_pairs={{0,16},{1,3},{2,18},{3,1},{4,20},{5,7},{6,22},{7,5},{8,24},{9,11},... | collective-permute-start | bytes 1327112 | tf_op jit(solution)/shard_map/ppermute | solution.py:75
  57.7 13.1 %collective-permute-start.3 = (bf16[192,2304]{1,0:T(8,128)(2,1)S(1)}, bf16[192,2304]{1,0:T(8,128)(2,1)S(1)}, u32[]{:S(2)}, u32[]{:S(2)}) collective-permute-start(bf16[192,2304]{1,0:T(8,128)(2,1)S(1)} %pad_maximum_fusion), channel_id=1, source_target_pairs={{0,2},{1,17},{2,0},{3,19},{4,6},{5,21},{6,4},{7,23},{8,10},{9,25},... | collective-permute-start | bytes 2654216 | tf_op jit(solution)/shard_map/ppermute | solution.py:75
  70.9 3.8 %copy-start = (bf16[384,2304]{1,0:T(8,128)(2,1)}, bf16[384,2304]{1,0:T(8,128)(2,1)S(1)}, u32[]{:S(2)}) copy-start(bf16[384,2304]{1,0:T(8,128)(2,1)S(1)} %constant_dynamic-update-slice_fusion) | copy-start | bytes 5308420
  70.9 3.8 %collective-permute-start.4 = (bf16[384,2304]{1,0:T(8,128)(2,1)S(1)}, bf16[384,2304]{1,0:T(8,128)(2,1)S(1)}, u32[]{:S(2)}, u32[]{:S(2)}) collective-permute-start(bf16[384,2304]{1,0:T(8,128)(2,1)S(1)} %constant_dynamic-update-slice_fusion), channel_id=1, source_target_pairs={{0,1},{1,0},{2,3},{3,2},{4,5},{5,4},{6,7},{7,6},{8,9},{9,8},{10,11... | collective-permute-start | bytes 5308424 | tf_op jit(solution)/shard_map/ppermute | solution.py:75
  74.6 1.2 copy-start.2
  161.9 9.2 %collective-permute-start.5 = (bf16[2,384,3456]{2,1,0:T(8,128)(2,1)}, bf16[2,384,3456]{2,1,0:T(8,128)(2,1)}, u32[]{:S(2)}, u32[]{:S(2)}) collective-permute-start(bf16[2,384,3456]{2,1,0:T(8,128)(2,1)} %get-tuple-element.89), channel_id=1, source_target_pairs={{0,1},{1,0},{2,3},{3,2},{4,5},{5,4},{6,7},{7,6},{8,9},{9,8},{10,11... | collective-permute-start | bytes 15925256 | tf_op jit(solution)/shard_map/ppermute | solution.py:75
  175.7 35.2 %collective-permute-start.7 = (bf16[2,192,3456]{2,1,0:T(8,128)(2,1)}, bf16[2,192,3456]{2,1,0:T(8,128)(2,1)S(1)}, u32[]{:S(2)}, u32[]{:S(2)}) collective-permute-start(bf16[2,192,3456]{2,1,0:T(8,128)(2,1)} %add_convert_fusion), channel_id=1, source_target_pairs={{0,2},{1,17},{2,0},{3,19},{4,6},{5,21},{6,4},{7,23},{8,10},{9,25},... | collective-permute-start | bytes 7962632 | tf_op jit(solution)/shard_map/ppermute | solution.py:75
  192.4 4.0 %collective-permute-start.6 = (bf16[384,2304]{1,0:T(8,128)(2,1)}, bf16[384,2304]{1,0:T(8,128)(2,1)}, u32[]{:S(2)}, u32[]{:S(2)}) collective-permute-start(bf16[384,2304]{1,0:T(8,128)(2,1)} %get-tuple-element.99), channel_id=1, source_target_pairs={{0,1},{1,0},{2,3},{3,2},{4,5},{5,4},{6,7},{7,6},{8,9},{9,8},{10,11... | collective-permute-start | bytes 5308424 | tf_op jit(solution)/shard_map/ppermute | solution.py:75
  199.0 23.5 %collective-permute-start.8 = (bf16[192,2304]{1,0:T(8,128)(2,1)}, bf16[192,2304]{1,0:T(8,128)(2,1)S(1)}, u32[]{:S(2)}, u32[]{:S(2)}) collective-permute-start(bf16[192,2304]{1,0:T(8,128)(2,1)} %add_convert_fusion.2), channel_id=1, source_target_pairs={{0,4},{1,9},{2,6},{3,11},{4,0},{5,13},{6,2},{7,15},{8,12},{9,1},{1... | collective-permute-start | bytes 2654216 | tf_op jit(solution)/shard_map/ppermute | solution.py:75
  210.9 3.9 %copy-start.5 = (f32[32,4,24]{2,1,0:T(4,128)S(1)}, f32[32,4,24]{2,1,0:T(4,128)}, u32[]{:S(2)}) copy-start(f32[32,4,24]{2,1,0:T(4,128)} %reshape_squeeze.3) | copy-start | bytes 36868
  210.9 4.5 %copy-start.9 = (f32[16,768]{1,0:T(8,128)S(1)}, f32[16,768]{1,0:T(8,128)}, u32[]{:S(2)}) copy-start(f32[16,768]{1,0:T(8,128)} %get-tuple-element.107) | copy-start | bytes 147460
  210.9 4.5 %copy-start.10 = (f32[16,768]{1,0:T(8,128)S(1)}, f32[16,768]{1,0:T(8,128)}, u32[]{:S(2)}) copy-start(f32[16,768]{1,0:T(8,128)} %get-tuple-element.106) | copy-start | bytes 147460
  214.2 18.9 %collective-permute-start.10 = (bf16[2,96,3456]{2,1,0:T(8,128)(2,1)}, bf16[2,96,3456]{2,1,0:T(8,128)(2,1)}, u32[]{:S(2)}, u32[]{:S(2)}) collective-permute-start(bf16[2,96,3456]{2,1,0:T(8,128)(2,1)} %add_convert_fusion.1), channel_id=1, source_target_pairs={{0,16},{1,3},{2,18},{3,1},{4,20},{5,7},{6,22},{7,5},{8,24},{9,11},... | collective-permute-start | bytes 3981320 | tf_op jit(solution)/shard_map/ppermute | solution.py:75
  222.5 15.7 %copy-start.3 = (bf16[192,2304]{1,0:T(8,128)(2,1)}, bf16[192,2304]{1,0:T(8,128)(2,1)S(1)}, u32[]{:S(2)}) copy-start(bf16[192,2304]{1,0:T(8,128)(2,1)S(1)} %collective-permute-done.8) | copy-start | bytes 2654212
  224.2 14.1 %collective-permute-start.9 = (bf16[96,2304]{1,0:T(8,128)(2,1)S(1)}, bf16[96,2304]{1,0:T(8,128)(2,1)}, u32[]{:S(2)}, u32[]{:S(2)}) collective-permute-start(bf16[96,2304]{1,0:T(8,128)(2,1)S(1)} %add_convert_fusion.4), channel_id=1, source_target_pairs={{0,8},{1,5},{2,10},{3,7},{4,12},{5,1},{6,14},{7,3},{8,0},{9,13},{1... | collective-permute-start | bytes 1327112 | tf_op jit(solution)/shard_map/ppermute | solution.py:75
  233.0 7.2 %copy-start.7 = (f32[16,768]{1,0:T(8,128)S(1)}, f32[16,768]{1,0:T(8,128)}, u32[]{:S(2)}) copy-start(f32[16,768]{1,0:T(8,128)} %table_grad.2) | copy-start | bytes 147460
  233.0 7.2 %copy-start.8 = (f32[16,768]{1,0:T(8,128)S(1)}, f32[16,768]{1,0:T(8,128)}, u32[]{:S(2)}) copy-start(f32[16,768]{1,0:T(8,128)} %table_grad.3) | copy-start | bytes 147460
  235.8 21.8 %collective-permute-start.12 = (bf16[2,48,3456]{2,1,0:T(8,128)(2,1)}, bf16[2,48,3456]{2,1,0:T(8,128)(2,1)}, u32[]{:S(2)}, u32[]{:S(2)}) collective-permute-start(bf16[2,48,3456]{2,1,0:T(8,128)(2,1)} %add_convert_fusion.3), channel_id=1, source_target_pairs={{0,4},{1,9},{2,6},{3,11},{4,0},{5,13},{6,2},{7,15},{8,12},{9,1},{1... | collective-permute-start | bytes 1990664 | tf_op jit(solution)/shard_map/ppermute | solution.py:75
  242.6 13.4 %all-to-all-start.1 = ((f32[32,1,624]{2,1,0:T(1,128)}), f32[32,1,624]{2,1,0:T(1,128)S(1)}, u32[]{:S(2)}, u32[]{:S(2)}) async-start(f32[32,1,624]{2,1,0:T(1,128)} %reshape.169), calls=%async_computation.1 | async-start | bytes 163840 | tf_op jit(solution)/shard_map/all_to_all | solution.py:1077
  245.9 14.6 %collective-permute-start.11 = (bf16[48,2304]{1,0:T(8,128)(2,1)}, bf16[48,2304]{1,0:T(8,128)(2,1)}, u32[]{:S(2)}, u32[]{:S(2)}) collective-permute-start(bf16[48,2304]{1,0:T(8,128)(2,1)} %add_convert_fusion.6), channel_id=1, source_target_pairs={{0,2},{1,17},{2,0},{3,19},{4,6},{5,21},{6,4},{7,23},{8,10},{9,25},... | collective-permute-start | bytes 663560 | tf_op jit(solution)/shard_map/ppermute | solution.py:75
  259.9 11.8 %collective-permute-start.14 = (bf16[2,24,3456]{2,1,0:T(8,128)(2,1)}, bf16[2,24,3456]{2,1,0:T(8,128)(2,1)S(1)}, u32[]{:S(2)}, u32[]{:S(2)}) collective-permute-start(bf16[2,24,3456]{2,1,0:T(8,128)(2,1)} %add_convert_fusion.5), channel_id=1, source_target_pairs={{0,8},{1,5},{2,10},{3,7},{4,12},{5,1},{6,14},{7,3},{8,0},{9,13},{1... | collective-permute-start | bytes 995336 | tf_op jit(solution)/shard_map/ppermute | solution.py:75
  262.3 11.7 %collective-permute-start.13 = (bf16[24,2304]{1,0:T(8,128)(2,1)}, bf16[24,2304]{1,0:T(8,128)(2,1)S(1)}, u32[]{:S(2)}, u32[]{:S(2)}) collective-permute-start(bf16[24,2304]{1,0:T(8,128)(2,1)} %add_convert_fusion.7), channel_id=1, source_target_pairs={{0,16},{1,3},{2,18},{3,1},{4,20},{5,7},{6,22},{7,5},{8,24},{9,11},... | collective-permute-start | bytes 331784 | tf_op jit(solution)/shard_map/ppermute | solution.py:75
Sparse Core Ops, SparseCore 0:
  10.9 98.3 all-gather.1

commit v2 on v1

--- a/solution.py
+++ b/solution.py
@@ -559,6 +559,10 @@
 
 def column_sum(ref, row, values):
     ref[row : row + 1, :] = jnp.sum(values, axis=0, keepdims=True)
+
+
+def add_column_sum(ref, row, values):
+    ref[row : row + 1, :] += jnp.sum(values, axis=0, keepdims=True)
 
 
 class Late:
@@ -668,31 +672,35 @@
     @pl.when(step == last)
     def _():
         late.wait()
-        cot = cb_s[...].astype(F32)
         sums_ref[...] = jnp.zeros_like(sums_ref)
-        normed, inverse = normal(after_s[...])
-        second = second_s[...]
-        column_sum(sums_ref, G_LN2_G, second * normed)
-        column_sum(sums_ref, G_LN2_B, second)
-        scaled = second * vec_ref[LN2_G : LN2_G + 1, :]
-        inner = jnp.mean(scaled, axis=-1, keepdims=True)
-        along = jnp.mean(scaled * normed, axis=-1, keepdims=True)
-        after_grad = cot + inverse * (scaled - inner - normed * along)
-        after_grad_ref[...] = after_grad
-        column_sum(sums_ref, G_GAM_A, after_grad * branch_s[...])
-        low = (vec_ref[GAM_A : GAM_A + 1, :] * after_grad).astype(BF16)
-        column_sum(sums_ref, G_OUT_B, low.astype(F32))
-        mixed_grad_ref[...] = nn(low, out_w_ref[...]).astype(BF16)
-        low_s[...] = low
+
+        def finish(here):
+            cot = cb_s[here, :].astype(F32)
+            normed, inverse = normal(after_s[here, :])
+            second = second_s[here, :]
+            add_column_sum(sums_ref, G_LN2_G, second * normed)
+            add_column_sum(sums_ref, G_LN2_B, second)
+            scaled = second * vec_ref[LN2_G : LN2_G + 1, :]
+            inner = jnp.mean(scaled, axis=-1, keepdims=True)
+            along = jnp.mean(scaled * normed, axis=-1, keepdims=True)
+            after_grad = cot + inverse * (scaled - inner - normed * along)
+            after_grad_ref[here, :] = after_grad
+            add_column_sum(sums_ref, G_GAM_A, after_grad * branch_s[here, :])
+            low = (vec_ref[GAM_A : GAM_A + 1, :] * after_grad).astype(BF16)
+            low_s[here, :] = low
+            add_column_sum(sums_ref, G_OUT_B, low.astype(F32))
+            mixed_grad_ref[here, :] = nn(low, out_w_ref[...]).astype(BF16)
+            branch = ff_s[here, :] + vec_ref[FC2_B : FC2_B + 1, :]
+            add_column_sum(sums_ref, G_GAM_M, cot * branch)
+            add_column_sum(sums_ref, G_FC2_B, up_ref[here, :].astype(F32))
+            cb_s[here, :] = (after_s[here, :] + vec_ref[GAM_M : GAM_M + 1, :] * branch).astype(BF16)
+
+        in_chunks(rows, rows // 4, finish)
         turn_low()
         in_chunks(half, half // 2, put_out_grad)
-        branch = ff_s[...] + vec_ref[FC2_B : FC2_B + 1, :]
-        result = (after_s[...] + vec_ref[GAM_M : GAM_M + 1, :] * branch).astype(BF16)
-        out_ref[...] = restore_rows(info[0], result, block_rows, image, out_ref.shape[0]).astype(
-            BF16
-        )
-        column_sum(sums_ref, G_GAM_M, cot * branch)
-        column_sum(sums_ref, G_FC2_B, up_ref[...].astype(F32))
+        out_ref[...] = restore_rows(
+            info[0], cb_s[...], block_rows, image, out_ref.shape[0]
+        ).astype(BF16)
 
 
 def feed(
@@ -823,6 +831,7 @@
     normed_s,
     inv_s,
     after_grad_s,
+    result_s,
     sems,
 ):
     step = pl.program_id(0)
@@ -844,18 +853,22 @@
     def _():
         late.wait()
         column_sum(sums_ref, G_V_B, packed_ref[...].astype(F32))
-        first = first_s[...]
-        normed = normed_s[...]
-        column_sum(sums_ref, G_LN1_G, first * normed)
-        column_sum(sums_ref, G_LN1_B, first)
-        scaled = first * vec_ref[LN1_G : LN1_G + 1, :]
-        inner = jnp.mean(scaled, axis=-1, keepdims=True)
-        along = jnp.mean(scaled * normed, axis=-1, keepdims=True)
-        back = inv_s[:, :1] * (scaled - inner - normed * along)
-        result = (after_grad_s[...] + back).astype(BF16)
-        out_ref[...] = restore_rows(info[0], result, block_rows, image, out_ref.shape[0]).astype(
-            BF16
-        )
+
+        def finish(here):
+            first = first_s[here, :]
+            normed = normed_s[here, :]
+            add_column_sum(sums_ref, G_LN1_G, first * normed)
+            add_column_sum(sums_ref, G_LN1_B, first)
+            scaled = first * vec_ref[LN1_G : LN1_G + 1, :]
+            inner = jnp.mean(scaled, axis=-1, keepdims=True)
+            along = jnp.mean(scaled * normed, axis=-1, keepdims=True)
+            back = inv_s[here, :1] * (scaled - inner - normed * along)
+            result_s[here, :] = (after_grad_s[here, :] + back).astype(BF16)
+
+        in_chunks(first_s.shape[0], first_s.shape[0] // 4, finish)
+        out_ref[...] = restore_rows(
+            info[0], result_s[...], block_rows, image, out_ref.shape[0]
+        ).astype(BF16)
 
 
 def input_grad(info, packed_grad, weights, vec, normed, inv, after_grad, image, block_rows, length):
@@ -883,6 +896,7 @@
             pltpu.VMEM((rows, width), F32),
             pltpu.VMEM((rows, 128), F32),
             pltpu.VMEM((rows, width), F32),
+            pltpu.VMEM((rows, width), BF16),
             pltpu.SemaphoreType.DMA((3,)),
         ],
         compiler_params=params(),
@@ -1024,7 +1038,7 @@
     qkv_full = qkv_full.reshape(width, -1)
     mixed, weights = attend(info, packed, table, block_rows)
     up, up_t, low_t = turn(order, qkv_order, vec, after(cb, mixed), low)
-    tile = 512
+    tile = 1024
     out, feed_keep, feed_send, fc1_sum, mixed_grad, after_grad, sums2 = feed(
         info,
         order,

time: 285 us -> 282 us (0.989)
  transfers between devices with their start and end apart: 18 -> 18, of which waited for: 11 -> 11; matrix products, arithmetic and copies ran while one was open for 13% -> 13% of each run, Pallas kernels for 33% -> 34%
where the time goes in v2:
time: 282 us; the launch traced here: 281 us
  Pallas kernels  145 us (51%)
  waiting for transfers between devices  52.3 us (19%)
  other arithmetic  32.8 us (12%)
  starting transfers between devices  24.2 us (9%)
  between operations  14.3 us (5%)
  local copies, waits for them, and re-layouts  13 us (5%)
    pallas_call x1, Pallas kernels, feed(): pl.pallas_call(functools.partial(feed_body, image, block_rows), grid=(ste...  50.2 us
    ppermute x15, waiting for transfers between devices, exchange(): lax.ppermute(values, AX, [(i, i ^ 1 << orders[i & 1][step]) for i in rang...  36.9 us
    convert_element_type x8, other arithmetic, scatter_step(): return (pieces, total(rows // 2, rows).astype(BF16))  20.9 us
    ppermute x15, starting transfers between devices, exchange(): lax.ppermute(values, AX, [(i, i ^ 1 << orders[i & 1][step]) for i in rang...  17 us
    pallas_call x2, Pallas kernels, attend_back(): pl.pallas_call(functools.partial(attend_back_body, block_rows, head_dim *...  16.7 us
    pallas_call x2, Pallas kernels, table_grad(): pl.pallas_call(functools.partial(table_grad_body, heads, groups), grid=(1...  14.6 us
    pallas_call x1, Pallas kernels, attend(): pl.pallas_call(functools.partial(attend_body, block_rows), grid=(pairs,),...  11.6 us
    pallas_call x1, Pallas kernels, input_grad(): pl.pallas_call(functools.partial(input_grad_body, image, block_rows), gri...  11 us
  transfers between devices with their start and end apart: 18, of which 11 were waited for; matrix products, arithmetic and copies ran while one was open for 13% of the time, Pallas kernels for 34%

profile of v2, /device:TPU:0, one launch (start us, length us, event | category | flops | bytes accessed | tf_op | source)
XLA Modules:
  0.0 281.2 jit_solution(1811997353280848878)
XLA Ops:
  7.2 1.8 pad_maximum_fusion.3
  9.0 4.1 %collective-permute-start = (bf16[24,2304]{1,0:T(8,128)(2,1)}, bf16[24,2304]{1,0:T(8,128)(2,1)S(1)}, u32[]{:S(2)}, u32[]{:S(2)}) collective-permute-start(bf16[24,2304]{1,0:T(8,128)(2,1)} %param.26), channel_id=1, source_target_pairs={{0,8},{1,5},{2,10},{3,7},{4,12},{5,1},{6,14},{7,3},{8,0},{9,13},{1... | collective-permute-start | bytes 331784 | tf_op jit(solution)/shard_map/ppermute | solution.py:75
  13.1 1.6 pack.1
  14.7 0.7 compare_reduce_fusion
  15.4 0.6 select_reduce_fusion.1
  16.0 1.9 pad_add_fusion.info
  17.9 7.4 %prepare.1 = (bf16[832,768]{1,0:T(8,128)(2,1)}, bf16[832,768]{1,0:T(8,128)(2,1)}, f32[832,768]{1,0:T(8,128)}, f32[832,128]{1,0:T(8,128)}) custom-call(s32[2]{0:T(128)} %pad_add_fusion.info, bf16[788,768]{1,0:T(8,128)(2,1)} %bitcast.42, bf16[788,768]{1,0:T(8,128)(2,1)} %bitcast.43), custom_call_target="tpu_custom_call" | custom-call | flops 80000000 | bytes 80000 | tf_op jit(solution)/shard_map/prepare/pallas_call | solution.py:220
  25.3 0.7 broadcast_in_dim.82
  26.0 3.8 %all-to-all-start = ((bf16[32,24,128]{2,1,0:T(8,128)(2,1)}), bf16[32,24,128]{2,1,0:T(8,128)(2,1)S(1)}, u32[]{:S(2)}, u32[]{:S(2)}) async-start(bf16[32,24,128]{2,1,0:T(8,128)(2,1)} %broadcast_in_dim.82), calls=%async_computation | async-start | bytes 393216 | tf_op jit(solution)/shard_map/all_to_all | solution.py:1034
  29.9 1.8 collective-permute-start.1
  31.7 8.6 %collective-permute-done.1 = bf16[48,2304]{1,0:T(8,128)(2,1)S(1)} collective-permute-done((bf16[48,2304]{1,0:T(8,128)(2,1)S(1)}, bf16[48,2304]{1,0:T(8,128)(2,1)S(1)}, u32[]{:S(2)}, u32[]{:S(2)}) %collective-permute-start.1) | collective-permute-done | bytes 221216 | tf_op jit(solution)/shard_map/ppermute | solution.py:75
  40.4 1.0 all-to-all-done
  41.4 0.7 collective-permute-start.2
  42.3 0.7 pad.4.index_ref
  43.0 9.1 %expand.1 = (f32[64,768]{1,0:T(8,128)}, f32[8,3072]{1,0:T(8,128)}, f32[12,208,256]{2,1,0:T(8,128)}) custom-call(bf16[768,128]{1,0:T(8,128)(2,1)} %bitcast.44, s32[208,256]{1,0:T(8,128)} %pad.4.index_ref), custom_call_target="tpu_custom_call" | custom-call | flops 100000000 | bytes 80000 | tf_op jit(solution)/shard_map/expand/pallas_call | solution.py:289
  52.1 5.5 %collective-permute-done.2 = bf16[96,2304]{1,0:T(8,128)(2,1)S(1)} collective-permute-done((bf16[96,2304]{1,0:T(8,128)(2,1)S(1)}, bf16[96,2304]{1,0:T(8,128)(2,1)S(1)}, u32[]{:S(2)}, u32[]{:S(2)}) %collective-permute-start.2) | collective-permute-done | bytes 442400 | tf_op jit(solution)/shard_map/ppermute | solution.py:75
  57.9 12.9 %collective-permute-done.3 = bf16[192,2304]{1,0:T(8,128)(2,1)S(1)} collective-permute-done((bf16[192,2304]{1,0:T(8,128)(2,1)S(1)}, bf16[192,2304]{1,0:T(8,128)(2,1)S(1)}, u32[]{:S(2)}, u32[]{:S(2)}) %collective-permute-start.3) | collective-permute-done | bytes 884768 | tf_op jit(solution)/shard_map/ppermute | solution.py:75
  71.0 0.6 broadcast_multiply_fusion
  71.7 0.9 add.201.order_ref
  72.7 0.9 add.202.qkv_order_ref
  73.6 1.0 collective-permute-done.4
  74.6 1.2 copy-done.2
  75.9 9.2 %project.1 = (bf16[832,2304]{1,0:T(8,128)(2,1)}, bf16[832,768]{1,0:T(8,128)(2,1)}, bf16[32,24,2304]{2,1,0:T(8,128)(2,1)}) custom-call(s32[32]{0:T(128)} %get-tuple-element.166.owners, f32[832,768]{1,0:T(8,128)} %get-tuple-element.69.normed_ref.normed_any, f32[64,768]{1,0:T(8,128)} %get-tuple-element.72.vec_ref, bf16[16,24,2304]{2,1,0:T(8,128)(2,1)} %bitcast.37, ...), custom_call_target="tpu_custom_call" | custom-call | flops 80000000 | bytes 80000 | tf_op jit(solution)/shard_map/project/pallas_call | solution.py:365
  85.1 11.6 %attend.1 = (bf16[832,768]{1,0:T(8,128)(2,1)}, f32[12,4,208,208]{3,2,1,0:T(8,128)}) custom-call(s32[2]{0:T(128)} %pad_add_fusion.info, bf16[832,2304]{1,0:T(8,128)(2,1)} %get-tuple-element.77.q_ref.k_ref.v_ref, bf16[832,2304]{1,0:T(8,128)(2,1)} %get-tuple-element.77.q_ref.k_ref.v_ref, bf16[832,2304]{1,0:T(8,128)(2,1)} %get-tuple-element.77.q_ref.k_ref.v_ref, ...), custom_call_target="tpu_custom_call" | custom-call | flops 120000000 | bytes 80000 | tf_op jit(solution)/shard_map/attend/pallas_call | solution.py:458
  96.7 6.3 %turn.1 = (bf16[832,768]{1,0:T(8,128)(2,1)}, bf16[768,832]{1,0:T(8,128)(2,1)}, bf16[768,832]{1,0:T(8,128)(2,1)}) custom-call(s32[768,1]{1,0:T(8,128)} %add.201.order_ref, s32[768,1]{1,0:T(8,128)} %add.202.qkv_order_ref, f32[64,768]{1,0:T(8,128)} %get-tuple-element.72.vec_ref, bf16[832,768]{1,0:T(8,128)(2,1)} %get-tuple-element.80.cb_ref.cb_any, ...), custom_call_target="tpu_custom_call" | custom-call | flops 60000000 | bytes 80000 | tf_op jit(solution)/shard_map/turn/pallas_call | solution.py:404
  103.0 6.3 %all-gather.2.cloned.1.call-done.out_w_ref.fc1_ref.fc2_ref = bf16[768,6912]{1,0:T(8,128)(2,1)} async-done(((bf16[24,6912]{1,0:T(8,128)(2,1)}), bf16[768,6912]{1,0:T(8,128)(2,1)}) %all-gather.2.cloned.1.call-update) | async-done | bytes 10616848 | tf_op jit(solution)/shard_map/all_gather | solution.py:1028
  109.3 50.2 %feed.1 = (bf16[788,768]{1,0:T(8,128)(2,1)}, bf16[2,384,3456]{2,1,0:T(8,128)(2,1)}, bf16[2,384,3456]{2,1,0:T(8,128)(2,1)}, f32[8,3072]{1,0:T(8,128)}, bf16[832,7...) custom-call(s32[2]{0:T(128)} %pad_add_fusion.info, s32[768,1]{1,0:T(8,128)} %add.201.order_ref, ...), custom_call_target="tpu_custom_call" | custom-call | flops 560000000 | bytes 80000 | tf_op jit(solution)/shard_map/feed/pallas_call | solution.py:734
  159.9 8.3 %attend_back.2 = (bf16[3,832,768]{2,1,0:T(8,128)(2,1)}, f32[12,208,256]{2,1,0:T(8,128)}) custom-call(bf16[832,2304]{1,0:T(8,128)(2,1)} %get-tuple-element.77.q_ref.k_ref.v_ref, bf16[832,2304]{1,0:T(8,128)(2,1)} %get-tuple-element.77.q_ref.k_ref.v_ref, bf16[832,2304]{1,0:T(8,128)(2,1)} %get-tuple-element.77.q_ref.k_ref.v_ref, ...), custom_call_target="tpu_custom_call" | custom-call | flops 80000000 | bytes 80000 | tf_op jit(solution)/shard_map/attend_back/pallas_call | solution.py:516
  168.7 4.6 %add_convert_fusion = bf16[2,192,3456]{2,1,0:T(8,128)(2,1)} fusion(bf16[2,384,3456]{2,1,0:T(8,128)(2,1)} %collective-permute-done.5, bf16[2,384,3456]{2,1,0:T(8,128)(2,1)} %get-tuple-element.88), kind=kLoop, calls=%fused_computation | loop fusion | flops 5308416 | bytes 7962624 | tf_op jit(solution)/shard_map/convert_element_type | solution.py:116
  173.3 1.5 collective-permute-start.7
  174.8 8.3 %attend_back.3 = (bf16[3,832,768]{2,1,0:T(8,128)(2,1)}, f32[12,208,256]{2,1,0:T(8,128)}) custom-call(bf16[832,2304]{1,0:T(8,128)(2,1)} %get-tuple-element.77.q_ref.k_ref.v_ref, bf16[832,2304]{1,0:T(8,128)(2,1)} %get-tuple-element.77.q_ref.k_ref.v_ref, ...), custom_call_target="tpu_custom_call", output_to_operand_aliasing={{0}: (5, {}), {1}: (6, {})} | custom-call | flops 80000000 | bytes 80000 | tf_op jit(solution)/shard_map/attend_back/pallas_call | solution.py:516
  183.2 6.9 %weight_grad.1 = (bf16[384,2304]{1,0:T(8,128)(2,1)}, bf16[384,2304]{1,0:T(8,128)(2,1)}) custom-call(bf16[768,832]{1,0:T(8,128)(2,1)} %get-tuple-element.97.low_t_ref, bf16[3,832,768]{2,1,0:T(8,128)(2,1)} %get-tuple-element.94.packed_ref), custom_call_target="tpu_custom_call" | custom-call | flops 100000000 | bytes 80000 | tf_op jit(solution)/shard_map/weight_grad/pallas_call | solution.py:806
  190.1 0.9 slice_reduce_fusion.8
  191.0 0.8 reshape_squeeze.3
  191.7 2.4 collective-permute-done.6
  194.1 2.6 add_convert_fusion.2
  196.6 1.3 collective-permute-start.8
  197.9 11.0 %input_grad.1 = (bf16[788,768]{1,0:T(8,128)(2,1)}, f32[16,768]{1,0:T(8,128)}) custom-call(s32[2]{0:T(128)} %pad_add_fusion.info, bf16[3,832,768]{2,1,0:T(8,128)(2,1)} %get-tuple-element.94.packed_ref, bf16[768,2304]{1,0:T(8,128)(2,1)} %bitcast.36, f32[64,768]{1,0:T(8,128)} %get-tuple-element.72.vec_ref, f32[832,768]{1,0:T(8,128)} %get-tuple-element.69.normed_ref.normed_any, ...), custom_call_target="tpu_custom_call" | custom-call | flops 160000000 | bytes 80000 | tf_op jit(solution)/shard_map/input_grad/pallas_call | solution.py:877
  208.9 3.3 %add_convert_fusion.1 = bf16[2,96,3456]{2,1,0:T(8,128)(2,1)} fusion(bf16[2,192,3456]{2,1,0:T(8,128)(2,1)S(1)} %collective-permute-done.7, bf16[2,384,3456]{2,1,0:T(8,128)(2,1)} %collective-permute-done.5, bf16[2,384,3456]{2,1,0:T(8,128)(2,1)} %get-tuple-element.88), kind=kLoop, calls=%fused_computation.1 | loop fusion | flops 3981312 | bytes 5308416 | tf_op jit(solution)/shard_map/convert_element_type | solution.py:116
  213.4 7.1 %table_grad.2 = f32[16,768]{1,0:T(8,128)} custom-call(f32[12,208,256]{2,1,0:T(8,128)} %get-tuple-element.112.table_ref, s32[208,256]{1,0:T(8,128)} %pad.4.index_ref), custom_call_target="tpu_custom_call" | custom-call | flops 160000000 | bytes 80000 | tf_op jit(solution)/shard_map/table_grad/pallas_call | solution.py:961
  220.6 1.6 add_convert_fusion.4
  222.2 1.1 collective-permute-start.9
  223.3 7.5 %table_grad.3 = f32[16,768]{1,0:T(8,128)} custom-call(f32[12,208,256]{2,1,0:T(8,128)} %get-tuple-element.112.table_ref, s32[208,256]{1,0:T(8,128)} %pad.4.index_ref), custom_call_target="tpu_custom_call" | custom-call | flops 160000000 | bytes 80000 | tf_op jit(solution)/shard_map/table_grad/pallas_call | solution.py:961
  230.8 2.7 add_convert_fusion.3
  233.6 1.6 collective-permute-start.12
  235.2 1.1 collective-permute-done.9
  236.3 1.9 add_convert_fusion.6
  238.5 0.9 pad_maximum_fusion.2
  239.8 0.9 reshape.169
  240.7 3.3 %all-to-all-start.1 = ((f32[32,1,624]{2,1,0:T(1,128)}), f32[32,1,624]{2,1,0:T(1,128)S(1)}, u32[]{:S(2)}, u32[]{:S(2)}) async-start(f32[32,1,624]{2,1,0:T(1,128)} %reshape.169), calls=%async_computation.1 | async-start | bytes 163840 | tf_op jit(solution)/shard_map/all_to_all | solution.py:1091
  243.9 1.8 collective-permute-start.11
  245.8 8.1 %all-to-all-done.1 = f32[32,1,624]{2,1,0:T(1,128)S(1)} async-done(((f32[32,1,624]{2,1,0:T(1,128)}), f32[32,1,624]{2,1,0:T(1,128)S(1)}, u32[]{:S(2)}, u32[]{:S(2)}) %all-to-all-start.1) | async-done | bytes 79904 | tf_op jit(solution)/shard_map/all_to_all | solution.py:1091
  254.4 0.8 reduce.22
  255.4 2.3 add_convert_fusion.5
  258.3 1.8 add_convert_fusion.7
  260.2 1.4 collective-permute-start.13
  261.9 0.7 copy.63
  263.2 0.6 copy.62
  263.9 0.8 slice_reduce_fusion
  264.7 4.8 %collective-permute-done.14 = bf16[2,24,3456]{2,1,0:T(8,128)(2,1)S(1)} collective-permute-done((bf16[2,24,3456]{2,1,0:T(8,128)(2,1)}, bf16[2,24,3456]{2,1,0:T(8,128)(2,1)S(1)}, u32[]{:S(2)}, u32[]{:S(2)}) %collective-permute-start.14) | collective-permute-done | bytes 331808 | tf_op jit(solution)/shard_map/ppermute | solution.py:75
  269.5 1.5 convert_add_fusion
  271.0 0.9 slice_bitcast_fusion
  271.9 1.9 convert_add_fusion.1
  273.7 0.6 maximum_bitcast_fusion
  (66 shorter events, 5.8 us)
Async XLA Ops:
  7.2 102.1 %all-gather.2.cloned.1.call-start = ((), (), s32[]{:S(2)}) async-start(), calls=%async_computation.2 | async-start | bytes 10948608 | tf_op jit(solution)/shard_map/all_gather | solution.py:1028
  9.0 20.9 %copy-start.1 = (bf16[24,2304]{1,0:T(8,128)(2,1)S(1)}, bf16[24,2304]{1,0:T(8,128)(2,1)}, u32[]{:S(2)}) copy-start(bf16[24,2304]{1,0:T(8,128)(2,1)} %param.26) | copy-start | bytes 331780
  9.0 20.8 %collective-permute-start = (bf16[24,2304]{1,0:T(8,128)(2,1)}, bf16[24,2304]{1,0:T(8,128)(2,1)S(1)}, u32[]{:S(2)}, u32[]{:S(2)}) collective-permute-start(bf16[24,2304]{1,0:T(8,128)(2,1)} %param.26), channel_id=1, source_target_pairs={{0,8},{1,5},{2,10},{3,7},{4,12},{5,1},{6,14},{7,3},{8,0},{9,13},{1... | collective-permute-start | bytes 331784 | tf_op jit(solution)/shard_map/ppermute | solution.py:75
  14.7 10.6 %copy-start.11 = (bf16[24,128]{1,0:T(8,128)(2,1)S(1)}, bf16[24,128]{1,0:T(8,128)(2,1)}, u32[]{:S(2)}) copy-start(bf16[24,128]{1,0:T(8,128)(2,1)} %pack.1) | copy-start | bytes 18436
  17.9 24.2 %copy-start.6 = (s32[197,197]{1,0:T(8,128)S(1)}, s32[197,197]{1,0:T(8,128)}, u32[]{:S(2)}) copy-start(s32[197,197]{1,0:T(8,128)} %param.23) | copy-start | bytes 465712
  26.0 15.4 %all-to-all-start = ((bf16[32,24,128]{2,1,0:T(8,128)(2,1)}), bf16[32,24,128]{2,1,0:T(8,128)(2,1)S(1)}, u32[]{:S(2)}, u32[]{:S(2)}) async-start(bf16[32,24,128]{2,1,0:T(8,128)(2,1)} %broadcast_in_dim.82), calls=%async_computation | async-start | bytes 393216 | tf_op jit(solution)/shard_map/all_to_all | solution.py:1034
  29.9 10.5 %collective-permute-start.1 = (bf16[48,2304]{1,0:T(8,128)(2,1)S(1)}, bf16[48,2304]{1,0:T(8,128)(2,1)S(1)}, u32[]{:S(2)}, u32[]{:S(2)}) collective-permute-start(bf16[48,2304]{1,0:T(8,128)(2,1)S(1)} %pad_maximum_fusion.4), channel_id=1, source_target_pairs={{0,4},{1,9},{2,6},{3,11},{4,0},{5,13},{6,2},{7,15},{8,12},{9,1},{1... | collective-permute-start | bytes 663560 | tf_op jit(solution)/shard_map/ppermute | solution.py:75
  41.4 1.6 copy-start.4
  41.4 16.2 %collective-permute-start.2 = (bf16[96,2304]{1,0:T(8,128)(2,1)S(1)}, bf16[96,2304]{1,0:T(8,128)(2,1)S(1)}, u32[]{:S(2)}, u32[]{:S(2)}) collective-permute-start(bf16[96,2304]{1,0:T(8,128)(2,1)S(1)} %pad_maximum_fusion.1), channel_id=1, source_target_pairs={{0,16},{1,3},{2,18},{3,1},{4,20},{5,7},{6,22},{7,5},{8,24},{9,11},... | collective-permute-start | bytes 1327112 | tf_op jit(solution)/shard_map/ppermute | solution.py:75
  57.7 13.1 %collective-permute-start.3 = (bf16[192,2304]{1,0:T(8,128)(2,1)S(1)}, bf16[192,2304]{1,0:T(8,128)(2,1)S(1)}, u32[]{:S(2)}, u32[]{:S(2)}) collective-permute-start(bf16[192,2304]{1,0:T(8,128)(2,1)S(1)} %pad_maximum_fusion), channel_id=1, source_target_pairs={{0,2},{1,17},{2,0},{3,19},{4,6},{5,21},{6,4},{7,23},{8,10},{9,25},... | collective-permute-start | bytes 2654216 | tf_op jit(solution)/shard_map/ppermute | solution.py:75
  70.9 3.8 %copy-start = (bf16[384,2304]{1,0:T(8,128)(2,1)}, bf16[384,2304]{1,0:T(8,128)(2,1)S(1)}, u32[]{:S(2)}) copy-start(bf16[384,2304]{1,0:T(8,128)(2,1)S(1)} %constant_dynamic-update-slice_fusion) | copy-start | bytes 5308420
  70.9 3.8 %collective-permute-start.4 = (bf16[384,2304]{1,0:T(8,128)(2,1)S(1)}, bf16[384,2304]{1,0:T(8,128)(2,1)S(1)}, u32[]{:S(2)}, u32[]{:S(2)}) collective-permute-start(bf16[384,2304]{1,0:T(8,128)(2,1)S(1)} %constant_dynamic-update-slice_fusion), channel_id=1, source_target_pairs={{0,1},{1,0},{2,3},{3,2},{4,5},{5,4},{6,7},{7,6},{8,9},{9,8},{10,11... | collective-permute-start | bytes 5308424 | tf_op jit(solution)/shard_map/ppermute | solution.py:75
  74.6 1.2 copy-start.2
  159.6 9.2 %collective-permute-start.5 = (bf16[2,384,3456]{2,1,0:T(8,128)(2,1)}, bf16[2,384,3456]{2,1,0:T(8,128)(2,1)}, u32[]{:S(2)}, u32[]{:S(2)}) collective-permute-start(bf16[2,384,3456]{2,1,0:T(8,128)(2,1)} %get-tuple-element.89), channel_id=1, source_target_pairs={{0,1},{1,0},{2,3},{3,2},{4,5},{5,4},{6,7},{7,6},{8,9},{9,8},{10,11... | collective-permute-start | bytes 15925256 | tf_op jit(solution)/shard_map/ppermute | solution.py:75
  173.3 35.6 %collective-permute-start.7 = (bf16[2,192,3456]{2,1,0:T(8,128)(2,1)}, bf16[2,192,3456]{2,1,0:T(8,128)(2,1)S(1)}, u32[]{:S(2)}, u32[]{:S(2)}) collective-permute-start(bf16[2,192,3456]{2,1,0:T(8,128)(2,1)} %add_convert_fusion), channel_id=1, source_target_pairs={{0,2},{1,17},{2,0},{3,19},{4,6},{5,21},{6,4},{7,23},{8,10},{9,25},... | collective-permute-start | bytes 7962632 | tf_op jit(solution)/shard_map/ppermute | solution.py:75
  190.1 4.0 %collective-permute-start.6 = (bf16[384,2304]{1,0:T(8,128)(2,1)}, bf16[384,2304]{1,0:T(8,128)(2,1)}, u32[]{:S(2)}, u32[]{:S(2)}) collective-permute-start(bf16[384,2304]{1,0:T(8,128)(2,1)} %get-tuple-element.99), channel_id=1, source_target_pairs={{0,1},{1,0},{2,3},{3,2},{4,5},{5,4},{6,7},{7,6},{8,9},{9,8},{10,11... | collective-permute-start | bytes 5308424 | tf_op jit(solution)/shard_map/ppermute | solution.py:75
  196.6 23.9 %collective-permute-start.8 = (bf16[192,2304]{1,0:T(8,128)(2,1)}, bf16[192,2304]{1,0:T(8,128)(2,1)S(1)}, u32[]{:S(2)}, u32[]{:S(2)}) collective-permute-start(bf16[192,2304]{1,0:T(8,128)(2,1)} %add_convert_fusion.2), channel_id=1, source_target_pairs={{0,4},{1,9},{2,6},{3,11},{4,0},{5,13},{6,2},{7,15},{8,12},{9,1},{1... | collective-permute-start | bytes 2654216 | tf_op jit(solution)/shard_map/ppermute | solution.py:75
  208.9 3.9 %copy-start.5 = (f32[32,4,24]{2,1,0:T(4,128)S(1)}, f32[32,4,24]{2,1,0:T(4,128)}, u32[]{:S(2)}) copy-start(f32[32,4,24]{2,1,0:T(4,128)} %reshape_squeeze.3) | copy-start | bytes 36868
  208.9 4.5 %copy-start.9 = (f32[16,768]{1,0:T(8,128)S(1)}, f32[16,768]{1,0:T(8,128)}, u32[]{:S(2)}) copy-start(f32[16,768]{1,0:T(8,128)} %get-tuple-element.107) | copy-start | bytes 147460
  208.9 4.5 %copy-start.10 = (f32[16,768]{1,0:T(8,128)S(1)}, f32[16,768]{1,0:T(8,128)}, u32[]{:S(2)}) copy-start(f32[16,768]{1,0:T(8,128)} %get-tuple-element.106) | copy-start | bytes 147460
  212.2 18.6 %collective-permute-start.10 = (bf16[2,96,3456]{2,1,0:T(8,128)(2,1)}, bf16[2,96,3456]{2,1,0:T(8,128)(2,1)}, u32[]{:S(2)}, u32[]{:S(2)}) collective-permute-start(bf16[2,96,3456]{2,1,0:T(8,128)(2,1)} %add_convert_fusion.1), channel_id=1, source_target_pairs={{0,16},{1,3},{2,18},{3,1},{4,20},{5,7},{6,22},{7,5},{8,24},{9,11},... | collective-permute-start | bytes 3981320 | tf_op jit(solution)/shard_map/ppermute | solution.py:75
  220.6 15.7 %copy-start.3 = (bf16[192,2304]{1,0:T(8,128)(2,1)}, bf16[192,2304]{1,0:T(8,128)(2,1)S(1)}, u32[]{:S(2)}) copy-start(bf16[192,2304]{1,0:T(8,128)(2,1)S(1)} %collective-permute-done.8) | copy-start | bytes 2654212
  222.2 14.1 %collective-permute-start.9 = (bf16[96,2304]{1,0:T(8,128)(2,1)S(1)}, bf16[96,2304]{1,0:T(8,128)(2,1)}, u32[]{:S(2)}, u32[]{:S(2)}) collective-permute-start(bf16[96,2304]{1,0:T(8,128)(2,1)S(1)} %add_convert_fusion.4), channel_id=1, source_target_pairs={{0,8},{1,5},{2,10},{3,7},{4,12},{5,1},{6,14},{7,3},{8,0},{9,13},{1... | collective-permute-start | bytes 1327112 | tf_op jit(solution)/shard_map/ppermute | solution.py:75
  230.8 7.4 %copy-start.7 = (f32[16,768]{1,0:T(8,128)S(1)}, f32[16,768]{1,0:T(8,128)}, u32[]{:S(2)}) copy-start(f32[16,768]{1,0:T(8,128)} %table_grad.2) | copy-start | bytes 147460
  230.8 7.4 %copy-start.8 = (f32[16,768]{1,0:T(8,128)S(1)}, f32[16,768]{1,0:T(8,128)}, u32[]{:S(2)}) copy-start(f32[16,768]{1,0:T(8,128)} %table_grad.3) | copy-start | bytes 147460
  233.6 21.9 %collective-permute-start.12 = (bf16[2,48,3456]{2,1,0:T(8,128)(2,1)}, bf16[2,48,3456]{2,1,0:T(8,128)(2,1)}, u32[]{:S(2)}, u32[]{:S(2)}) collective-permute-start(bf16[2,48,3456]{2,1,0:T(8,128)(2,1)} %add_convert_fusion.3), channel_id=1, source_target_pairs={{0,4},{1,9},{2,6},{3,11},{4,0},{5,13},{6,2},{7,15},{8,12},{9,1},{1... | collective-permute-start | bytes 1990664 | tf_op jit(solution)/shard_map/ppermute | solution.py:75
  240.7 13.2 %all-to-all-start.1 = ((f32[32,1,624]{2,1,0:T(1,128)}), f32[32,1,624]{2,1,0:T(1,128)S(1)}, u32[]{:S(2)}, u32[]{:S(2)}) async-start(f32[32,1,624]{2,1,0:T(1,128)} %reshape.169), calls=%async_computation.1 | async-start | bytes 163840 | tf_op jit(solution)/shard_map/all_to_all | solution.py:1091
  243.9 14.4 %collective-permute-start.11 = (bf16[48,2304]{1,0:T(8,128)(2,1)}, bf16[48,2304]{1,0:T(8,128)(2,1)}, u32[]{:S(2)}, u32[]{:S(2)}) collective-permute-start(bf16[48,2304]{1,0:T(8,128)(2,1)} %add_convert_fusion.6), channel_id=1, source_target_pairs={{0,2},{1,17},{2,0},{3,19},{4,6},{5,21},{6,4},{7,23},{8,10},{9,25},... | collective-permute-start | bytes 663560 | tf_op jit(solution)/shard_map/ppermute | solution.py:75
  257.7 11.8 %collective-permute-start.14 = (bf16[2,24,3456]{2,1,0:T(8,128)(2,1)}, bf16[2,24,3456]{2,1,0:T(8,128)(2,1)S(1)}, u32[]{:S(2)}, u32[]{:S(2)}) collective-permute-start(bf16[2,24,3456]{2,1,0:T(8,128)(2,1)} %add_convert_fusion.5), channel_id=1, source_target_pairs={{0,8},{1,5},{2,10},{3,7},{4,12},{5,1},{6,14},{7,3},{8,0},{9,13},{1... | collective-permute-start | bytes 995336 | tf_op jit(solution)/shard_map/ppermute | solution.py:75
  260.2 11.7 %collective-permute-start.13 = (bf16[24,2304]{1,0:T(8,128)(2,1)}, bf16[24,2304]{1,0:T(8,128)(2,1)S(1)}, u32[]{:S(2)}, u32[]{:S(2)}) collective-permute-start(bf16[24,2304]{1,0:T(8,128)(2,1)} %add_convert_fusion.7), channel_id=1, source_target_pairs={{0,16},{1,3},{2,18},{3,1},{4,20},{5,7},{6,22},{7,5},{8,24},{9,11},... | collective-permute-start | bytes 331784 | tf_op jit(solution)/shard_map/ppermute | solution.py:75
Sparse Core Ops, SparseCore 0:
  10.9 98.3 all-gather.1

commit v3 on v2

--- a/solution.py
+++ b/solution.py
@@ -147,13 +147,31 @@
     return one
 
 
-def restore_rows(first, blocked, block_rows, image, length):
+def restore_body(image, block_rows, info, *refs):
+    sources, targets = refs[: len(refs) // 2], refs[len(refs) // 2 :]
+    length = targets[0].shape[0]
     lanes = lax.broadcasted_iota(jnp.int32, (1, block_rows), 1)
     wanted = jnp.concatenate(
-        [block_source(first, number, lanes, image, length) for number in range(IMGS)], axis=1
+        [block_source(info[0], number, lanes, image, length) for number in range(IMGS)], axis=1
     )
     rows = lax.broadcasted_iota(jnp.int32, (length, IMGS * block_rows), 0)
-    return nn((rows == wanted).astype(BF16), blocked)
+    back = (rows == wanted).astype(BF16)
+    for source, target in zip(sources, targets, strict=True):
+        target[...] = nn(back, source[...]).astype(BF16)
+
+
+def restore(info, image, block_rows, length, *blocked):
+    rows, width = blocked[0].shape
+    return pl.pallas_call(
+        functools.partial(restore_body, image, block_rows),
+        grid=(1,),
+        in_specs=[smem()] + [full((rows, width))] * len(blocked),
+        out_specs=[full((length, width))] * len(blocked),
+        out_shape=[jax.ShapeDtypeStruct((length, width), BF16)] * len(blocked),
+        compiler_params=params(),
+        cost_estimate=cost(4),
+        name="restore",
+    )(info, *blocked)
 
 
 def pack_body(bias_at, table_at, ratio, bias_ref, table_ref, *rest):
@@ -693,14 +711,11 @@
             branch = ff_s[here, :] + vec_ref[FC2_B : FC2_B + 1, :]
             add_column_sum(sums_ref, G_GAM_M, cot * branch)
             add_column_sum(sums_ref, G_FC2_B, up_ref[here, :].astype(F32))
-            cb_s[here, :] = (after_s[here, :] + vec_ref[GAM_M : GAM_M + 1, :] * branch).astype(BF16)
+            out_ref[here, :] = (after_s[here, :] + vec_ref[GAM_M : GAM_M + 1, :] * branch).astype(BF16)
 
         in_chunks(rows, rows // 4, finish)
         turn_low()
         in_chunks(half, half // 2, put_out_grad)
-        out_ref[...] = restore_rows(
-            info[0], cb_s[...], block_rows, image, out_ref.shape[0]
-        ).astype(BF16)
 
 
 def feed(
@@ -749,7 +764,7 @@
         ]
         + [anywhere],
         out_specs=[
-            full((length, width)),
+            full((rows, width)),
             pl.BlockSpec((2, width // 2, tile), lambda i: (0, 0, i)),
             pl.BlockSpec((2, width // 2, tile), lambda i: (0, 0, i)),
             pl.BlockSpec((8, tile), lambda i: (0, at(i))),
@@ -758,7 +773,7 @@
             full((16, width)),
         ],
         out_shape=[
-            jax.ShapeDtypeStruct((length, width), BF16),
+            jax.ShapeDtypeStruct((rows, width), BF16),
             jax.ShapeDtypeStruct((2, width // 2, hidden + width // 2), BF16),
             jax.ShapeDtypeStruct((2, width // 2, hidden + width // 2), BF16),
             jax.ShapeDtypeStruct((8, hidden), F32),
@@ -831,7 +846,6 @@
     normed_s,
     inv_s,
     after_grad_s,
-    result_s,
     sems,
 ):
     step = pl.program_id(0)
@@ -863,12 +877,9 @@
             inner = jnp.mean(scaled, axis=-1, keepdims=True)
             along = jnp.mean(scaled * normed, axis=-1, keepdims=True)
             back = inv_s[here, :1] * (scaled - inner - normed * along)
-            result_s[here, :] = (after_grad_s[here, :] + back).astype(BF16)
+            out_ref[here, :] = (after_grad_s[here, :] + back).astype(BF16)
 
         in_chunks(first_s.shape[0], first_s.shape[0] // 4, finish)
-        out_ref[...] = restore_rows(
-            info[0], result_s[...], block_rows, image, out_ref.shape[0]
-        ).astype(BF16)
 
 
 def input_grad(info, packed_grad, weights, vec, normed, inv, after_grad, image, block_rows, length):
@@ -886,9 +897,9 @@
             anywhere,
             anywhere,
         ],
-        out_specs=[full((length, width)), full((16, width))],
+        out_specs=[full((rows, width)), full((16, width))],
         out_shape=[
-            jax.ShapeDtypeStruct((length, width), BF16),
+            jax.ShapeDtypeStruct((rows, width), BF16),
             jax.ShapeDtypeStruct((16, width), F32),
         ],
         scratch_shapes=[
@@ -896,7 +907,6 @@
             pltpu.VMEM((rows, width), F32),
             pltpu.VMEM((rows, 128), F32),
             pltpu.VMEM((rows, width), F32),
-            pltpu.VMEM((rows, width), BF16),
             pltpu.SemaphoreType.DMA((3,)),
         ],
         compiler_params=params(),
@@ -1089,6 +1099,10 @@
     rows = jnp.concatenate([sums1[:10] + sums2[:10], slot_sums[:heads]], axis=0)
     rows = jnp.transpose(rows.reshape(-1, count, own), (1, 0, 2))
     swapped = lax.all_to_all(jnp.concatenate([rows, biases], axis=1), AX, 0, 0, tiled=True)
+    out, in_grad = restore(
+        info, image, block_rows, length, after(out, b_send), in_grad
+    )
+    swapped = after(swapped, out)
     a_pieces, a_send = scatter_step(0, a_pieces, a_send, 3, count, swapped)
     b_pieces, b_send = scatter_step(1, b_pieces, b_send, 3, count, a_send)
     late_send = b_send

time: 282 us -> 280 us (level)
  waiting for transfers between devices: 52.3 us -> 46.7 us
    pallas_call x0 -> x1, Pallas kernels: none -> 5.49 us  [restore(): pl.pallas_call(functools.partial(restore_body, image, block_rows), grid=(...]
    all_to_all x1, waiting for transfers between devices: 8.09 us -> 2.65 us  [local(): lax.all_to_all(jnp.concatenate([rows, biases], axis=1), AX, 0, 0, tiled=T...]
  transfers between devices with their start and end apart: 18 -> 18, of which waited for: 11 -> 12; matrix products, arithmetic and copies ran while one was open for 13% -> 13% of each run, Pallas kernels for 34% -> 35%
where the time goes in v3:
time: 280 us; the launch traced here: 279 us
  Pallas kernels  147 us (52%)
  waiting for transfers between devices  46.7 us (17%)
  other arithmetic  32.8 us (12%)
  starting transfers between devices  24.7 us (9%)
  between operations  14.3 us (5%)
  local copies, waits for them, and re-layouts  13 us (5%)
    pallas_call x1, Pallas kernels, feed(): pl.pallas_call(functools.partial(feed_body, image, block_rows), grid=(ste...  48.8 us
    ppermute x15, waiting for transfers between devices, exchange(): lax.ppermute(values, AX, [(i, i ^ 1 << orders[i & 1][step]) for i in rang...  35.6 us
    convert_element_type x8, other arithmetic, scatter_step(): return (pieces, total(rows // 2, rows).astype(BF16))  20.9 us
    ppermute x15, starting transfers between devices, exchange(): lax.ppermute(values, AX, [(i, i ^ 1 << orders[i & 1][step]) for i in rang...  17.4 us
    pallas_call x2, Pallas kernels, attend_back(): pl.pallas_call(functools.partial(attend_back_body, block_rows, head_dim *...  16.8 us
    pallas_call x2, Pallas kernels, table_grad(): pl.pallas_call(functools.partial(table_grad_body, heads, groups), grid=(1...  14.6 us
    pallas_call x1, Pallas kernels, attend(): pl.pallas_call(functools.partial(attend_body, block_rows), grid=(pairs,),...  11.6 us
    pallas_call x1, Pallas kernels, input_grad(): pl.pallas_call(functools.partial(input_grad_body, image, block_rows), gri...  9.64 us
  transfers between devices with their start and end apart: 18, of which 12 were waited for; matrix products, arithmetic and copies ran while one was open for 13% of the time, Pallas kernels for 35%

profile of v3, /device:TPU:0, one launch (start us, length us, event | category | flops | bytes accessed | tf_op | source)
XLA Modules:
  0.0 279.0 jit_solution(16945094939383082529)
XLA Ops:
  7.2 1.8 pad_maximum_fusion.3
  9.0 4.1 %collective-permute-start = (bf16[24,2304]{1,0:T(8,128)(2,1)}, bf16[24,2304]{1,0:T(8,128)(2,1)S(1)}, u32[]{:S(2)}, u32[]{:S(2)}) collective-permute-start(bf16[24,2304]{1,0:T(8,128)(2,1)} %param.26), channel_id=1, source_target_pairs={{0,8},{1,5},{2,10},{3,7},{4,12},{5,1},{6,14},{7,3},{8,0},{9,13},{1... | collective-permute-start | bytes 331784 | tf_op jit(solution)/shard_map/ppermute | solution.py:75
  13.1 1.6 pack.1
  14.7 0.7 compare_reduce_fusion
  15.4 0.6 select_reduce_fusion.1
  16.0 1.9 pad_add_fusion.info
  17.9 7.3 %prepare.1 = (bf16[832,768]{1,0:T(8,128)(2,1)}, bf16[832,768]{1,0:T(8,128)(2,1)}, f32[832,768]{1,0:T(8,128)}, f32[832,128]{1,0:T(8,128)}) custom-call(s32[2]{0:T(128)} %pad_add_fusion.info, bf16[788,768]{1,0:T(8,128)(2,1)} %bitcast.42, bf16[788,768]{1,0:T(8,128)(2,1)} %bitcast.43), custom_call_target="tpu_custom_call" | custom-call | flops 80000000 | bytes 80000 | tf_op jit(solution)/shard_map/prepare/pallas_call | solution.py:238
  25.2 0.7 broadcast_in_dim.82
  25.9 3.8 %all-to-all-start = ((bf16[32,24,128]{2,1,0:T(8,128)(2,1)}), bf16[32,24,128]{2,1,0:T(8,128)(2,1)S(1)}, u32[]{:S(2)}, u32[]{:S(2)}) async-start(bf16[32,24,128]{2,1,0:T(8,128)(2,1)} %broadcast_in_dim.82), calls=%async_computation | async-start | bytes 393216 | tf_op jit(solution)/shard_map/all_to_all | solution.py:1044
  29.8 1.8 collective-permute-start.1
  31.6 8.7 %collective-permute-done.1 = bf16[48,2304]{1,0:T(8,128)(2,1)S(1)} collective-permute-done((bf16[48,2304]{1,0:T(8,128)(2,1)S(1)}, bf16[48,2304]{1,0:T(8,128)(2,1)S(1)}, u32[]{:S(2)}, u32[]{:S(2)}) %collective-permute-start.1) | collective-permute-done | bytes 221216 | tf_op jit(solution)/shard_map/ppermute | solution.py:75
  40.3 0.9 all-to-all-done
  41.3 0.7 collective-permute-start.2
  42.2 0.7 pad.4.index_ref
  42.9 8.9 %expand.1 = (f32[64,768]{1,0:T(8,128)}, f32[8,3072]{1,0:T(8,128)}, f32[12,208,256]{2,1,0:T(8,128)}) custom-call(bf16[768,128]{1,0:T(8,128)(2,1)} %bitcast.44, s32[208,256]{1,0:T(8,128)} %pad.4.index_ref), custom_call_target="tpu_custom_call" | custom-call | flops 100000000 | bytes 80000 | tf_op jit(solution)/shard_map/expand/pallas_call | solution.py:307
  51.9 4.7 %collective-permute-done.2 = bf16[96,2304]{1,0:T(8,128)(2,1)S(1)} collective-permute-done((bf16[96,2304]{1,0:T(8,128)(2,1)S(1)}, bf16[96,2304]{1,0:T(8,128)(2,1)S(1)}, u32[]{:S(2)}, u32[]{:S(2)}) %collective-permute-start.2) | collective-permute-done | bytes 442400 | tf_op jit(solution)/shard_map/ppermute | solution.py:75
  56.6 0.8 collective-permute-start.3
  57.5 12.2 %collective-permute-done.3 = bf16[192,2304]{1,0:T(8,128)(2,1)S(1)} collective-permute-done((bf16[192,2304]{1,0:T(8,128)(2,1)S(1)}, bf16[192,2304]{1,0:T(8,128)(2,1)S(1)}, u32[]{:S(2)}, u32[]{:S(2)}) %collective-permute-start.3) | collective-permute-done | bytes 884768 | tf_op jit(solution)/shard_map/ppermute | solution.py:75
  70.6 0.9 add.201.order_ref
  71.6 0.9 add.202.qkv_order_ref
  72.5 1.0 collective-permute-done.4
  73.5 1.2 copy-done.2
  74.8 9.3 %project.1 = (bf16[832,2304]{1,0:T(8,128)(2,1)}, bf16[832,768]{1,0:T(8,128)(2,1)}, bf16[32,24,2304]{2,1,0:T(8,128)(2,1)}) custom-call(s32[32]{0:T(128)} %get-tuple-element.174.owners, f32[832,768]{1,0:T(8,128)} %get-tuple-element.73.normed_ref.normed_any, f32[64,768]{1,0:T(8,128)} %get-tuple-element.76.vec_ref, bf16[16,24,2304]{2,1,0:T(8,128)(2,1)} %bitcast.37, ...), custom_call_target="tpu_custom_call" | custom-call | flops 80000000 | bytes 80000 | tf_op jit(solution)/shard_map/project/pallas_call | solution.py:383
  84.1 11.6 %attend.1 = (bf16[832,768]{1,0:T(8,128)(2,1)}, f32[12,4,208,208]{3,2,1,0:T(8,128)}) custom-call(s32[2]{0:T(128)} %pad_add_fusion.info, bf16[832,2304]{1,0:T(8,128)(2,1)} %get-tuple-element.81.q_ref.k_ref.v_ref, bf16[832,2304]{1,0:T(8,128)(2,1)} %get-tuple-element.81.q_ref.k_ref.v_ref, bf16[832,2304]{1,0:T(8,128)(2,1)} %get-tuple-element.81.q_ref.k_ref.v_ref, ...), custom_call_target="tpu_custom_call" | custom-call | flops 120000000 | bytes 80000 | tf_op jit(solution)/shard_map/attend/pallas_call | solution.py:476
  95.6 6.5 %turn.1 = (bf16[832,768]{1,0:T(8,128)(2,1)}, bf16[768,832]{1,0:T(8,128)(2,1)}, bf16[768,832]{1,0:T(8,128)(2,1)}) custom-call(s32[768,1]{1,0:T(8,128)} %add.201.order_ref, s32[768,1]{1,0:T(8,128)} %add.202.qkv_order_ref, f32[64,768]{1,0:T(8,128)} %get-tuple-element.76.vec_ref, bf16[832,768]{1,0:T(8,128)(2,1)} %get-tuple-element.84.cb_ref.cb_any, ...), custom_call_target="tpu_custom_call" | custom-call | flops 60000000 | bytes 80000 | tf_op jit(solution)/shard_map/turn/pallas_call | solution.py:422
  102.2 7.6 %all-gather.2.cloned.1.call-done.out_w_ref.fc1_ref.fc2_ref = bf16[768,6912]{1,0:T(8,128)(2,1)} async-done(((bf16[24,6912]{1,0:T(8,128)(2,1)}), bf16[768,6912]{1,0:T(8,128)(2,1)}) %all-gather.2.cloned.1.call-update) | async-done | bytes 10616848 | tf_op jit(solution)/shard_map/all_gather | solution.py:1038
  109.8 48.8 %feed.1 = (bf16[832,768]{1,0:T(8,128)(2,1)}, bf16[2,384,3456]{2,1,0:T(8,128)(2,1)}, bf16[2,384,3456]{2,1,0:T(8,128)(2,1)}, f32[8,3072]{1,0:T(8,128)}, bf16[832,7...) custom-call(s32[2]{0:T(128)} %pad_add_fusion.info, s32[768,1]{1,0:T(8,128)} %add.201.order_ref, ...), custom_call_target="tpu_custom_call" | custom-call | flops 560000000 | bytes 80000 | tf_op jit(solution)/shard_map/feed/pallas_call | solution.py:749
  158.9 8.4 %attend_back.2 = (bf16[3,832,768]{2,1,0:T(8,128)(2,1)}, f32[12,208,256]{2,1,0:T(8,128)}) custom-call(bf16[832,2304]{1,0:T(8,128)(2,1)} %get-tuple-element.81.q_ref.k_ref.v_ref, bf16[832,2304]{1,0:T(8,128)(2,1)} %get-tuple-element.81.q_ref.k_ref.v_ref, bf16[832,2304]{1,0:T(8,128)(2,1)} %get-tuple-element.81.q_ref.k_ref.v_ref, ...), custom_call_target="tpu_custom_call" | custom-call | flops 80000000 | bytes 80000 | tf_op jit(solution)/shard_map/attend_back/pallas_call | solution.py:534
  167.7 4.6 %add_convert_fusion = bf16[2,192,3456]{2,1,0:T(8,128)(2,1)} fusion(bf16[2,384,3456]{2,1,0:T(8,128)(2,1)} %collective-permute-done.5, bf16[2,384,3456]{2,1,0:T(8,128)(2,1)} %get-tuple-element.93), kind=kLoop, calls=%fused_computation | loop fusion | flops 5308416 | bytes 7962624 | tf_op jit(solution)/shard_map/convert_element_type | solution.py:116
  172.4 1.5 collective-permute-start.8
  173.8 8.4 %attend_back.3 = (bf16[3,832,768]{2,1,0:T(8,128)(2,1)}, f32[12,208,256]{2,1,0:T(8,128)}) custom-call(bf16[832,2304]{1,0:T(8,128)(2,1)} %get-tuple-element.81.q_ref.k_ref.v_ref, bf16[832,2304]{1,0:T(8,128)(2,1)} %get-tuple-element.81.q_ref.k_ref.v_ref, ...), custom_call_target="tpu_custom_call", output_to_operand_aliasing={{0}: (5, {}), {1}: (6, {})} | custom-call | flops 80000000 | bytes 80000 | tf_op jit(solution)/shard_map/attend_back/pallas_call | solution.py:534
  182.2 6.9 %weight_grad.1 = (bf16[384,2304]{1,0:T(8,128)(2,1)}, bf16[384,2304]{1,0:T(8,128)(2,1)}) custom-call(bf16[768,832]{1,0:T(8,128)(2,1)} %get-tuple-element.90.low_t_ref, bf16[3,832,768]{2,1,0:T(8,128)(2,1)} %get-tuple-element.99.packed_ref), custom_call_target="tpu_custom_call" | custom-call | flops 100000000 | bytes 80000 | tf_op jit(solution)/shard_map/weight_grad/pallas_call | solution.py:821
  189.2 0.9 slice_reduce_fusion.8
  190.1 0.8 reshape_squeeze.3
  190.8 2.4 collective-permute-done.6
  193.2 2.5 add_convert_fusion.2
  195.7 1.3 collective-permute-start.7
  197.0 9.6 %input_grad.1 = (bf16[832,768]{1,0:T(8,128)(2,1)}, f32[16,768]{1,0:T(8,128)}) custom-call(s32[2]{0:T(128)} %pad_add_fusion.info, bf16[3,832,768]{2,1,0:T(8,128)(2,1)} %get-tuple-element.99.packed_ref, bf16[768,2304]{1,0:T(8,128)(2,1)} %bitcast.36, f32[64,768]{1,0:T(8,128)} %get-tuple-element.76.vec_ref, f32[832,768]{1,0:T(8,128)} %get-tuple-element.73.normed_ref.normed_any, ...), custom_call_target="tpu_custom_call" | custom-call | flops 160000000 | bytes 80000 | tf_op jit(solution)/shard_map/input_grad/pallas_call | solution.py:888
  206.7 3.3 %add_convert_fusion.1 = bf16[2,96,3456]{2,1,0:T(8,128)(2,1)} fusion(bf16[2,192,3456]{2,1,0:T(8,128)(2,1)S(1)} %collective-permute-done.8, bf16[2,384,3456]{2,1,0:T(8,128)(2,1)} %collective-permute-done.5, bf16[2,384,3456]{2,1,0:T(8,128)(2,1)} %get-tuple-element.93), kind=kLoop, calls=%fused_computation.1 | loop fusion | flops 3981312 | bytes 5308416 | tf_op jit(solution)/shard_map/convert_element_type | solution.py:116
  211.2 7.1 %table_grad.2 = f32[16,768]{1,0:T(8,128)} custom-call(f32[12,208,256]{2,1,0:T(8,128)} %get-tuple-element.114.table_ref, s32[208,256]{1,0:T(8,128)} %pad.4.index_ref), custom_call_target="tpu_custom_call" | custom-call | flops 160000000 | bytes 80000 | tf_op jit(solution)/shard_map/table_grad/pallas_call | solution.py:971
  218.5 1.6 add_convert_fusion.4
  220.1 1.4 collective-permute-start.9
  221.5 7.5 %table_grad.3 = f32[16,768]{1,0:T(8,128)} custom-call(f32[12,208,256]{2,1,0:T(8,128)} %get-tuple-element.114.table_ref, s32[208,256]{1,0:T(8,128)} %pad.4.index_ref), custom_call_target="tpu_custom_call" | custom-call | flops 160000000 | bytes 80000 | tf_op jit(solution)/shard_map/table_grad/pallas_call | solution.py:971
  229.0 2.7 add_convert_fusion.3
  231.7 1.3 collective-permute-start.12
  233.0 1.2 collective-permute-done.9
  234.2 1.9 add_convert_fusion.6
  236.4 0.9 pad_maximum_fusion.2
  237.7 0.9 reshape.169
  238.6 3.4 %all-to-all-start.1 = ((f32[32,1,624]{2,1,0:T(1,128)}), f32[32,1,624]{2,1,0:T(1,128)S(1)}, u32[]{:S(2)}, u32[]{:S(2)}) async-start(f32[32,1,624]{2,1,0:T(1,128)} %reshape.169), calls=%async_computation.1 | async-start | bytes 163840 | tf_op jit(solution)/shard_map/all_to_all | solution.py:1101
  242.0 1.6 collective-permute-start.11
  243.5 5.5 %restore.1 = (bf16[788,768]{1,0:T(8,128)(2,1)}, bf16[788,768]{1,0:T(8,128)(2,1)}) custom-call(s32[2]{0:T(128)} %pad_add_fusion.info, bf16[832,768]{1,0:T(8,128)(2,1)} %get-tuple-element.117.refs_0_, bf16[832,768]{1,0:T(8,128)(2,1)} %get-tuple-element.110.refs_1_), custom_call_target="tpu_custom_call" | custom-call | flops 80000000 | bytes 80000 | tf_op jit(solution)/shard_map/restore/pallas_call | solution.py:165
  249.0 2.7 all-to-all-done.1
  252.2 0.8 reduce.22
  253.2 2.2 add_convert_fusion.5
  255.5 0.6 collective-permute-start.14
  256.1 1.8 add_convert_fusion.7
  257.9 1.4 collective-permute-start.13
  259.6 0.7 copy.63
  261.6 0.8 slice_reduce_fusion
  262.4 4.8 %collective-permute-done.14 = bf16[2,24,3456]{2,1,0:T(8,128)(2,1)S(1)} collective-permute-done((bf16[2,24,3456]{2,1,0:T(8,128)(2,1)}, bf16[2,24,3456]{2,1,0:T(8,128)(2,1)S(1)}, u32[]{:S(2)}, u32[]{:S(2)}) %collective-permute-start.14) | collective-permute-done | bytes 331808 | tf_op jit(solution)/shard_map/ppermute | solution.py:75
  267.2 1.5 convert_add_fusion
  268.8 0.9 slice_bitcast_fusion
  269.6 1.9 convert_add_fusion.1
  (67 shorter events, 7.0 us)
Async XLA Ops:
  7.2 102.6 %all-gather.2.cloned.1.call-start = ((), (), s32[]{:S(2)}) async-start(), calls=%async_computation.2 | async-start | bytes 10948608 | tf_op jit(solution)/shard_map/all_gather | solution.py:1038
  9.0 20.8 %copy-start.1 = (bf16[24,2304]{1,0:T(8,128)(2,1)S(1)}, bf16[24,2304]{1,0:T(8,128)(2,1)}, u32[]{:S(2)}) copy-start(bf16[24,2304]{1,0:T(8,128)(2,1)} %param.26) | copy-start | bytes 331780
  9.0 20.7 %collective-permute-start = (bf16[24,2304]{1,0:T(8,128)(2,1)}, bf16[24,2304]{1,0:T(8,128)(2,1)S(1)}, u32[]{:S(2)}, u32[]{:S(2)}) collective-permute-start(bf16[24,2304]{1,0:T(8,128)(2,1)} %param.26), channel_id=1, source_target_pairs={{0,8},{1,5},{2,10},{3,7},{4,12},{5,1},{6,14},{7,3},{8,0},{9,13},{1... | collective-permute-start | bytes 331784 | tf_op jit(solution)/shard_map/ppermute | solution.py:75
  14.7 10.5 %copy-start.11 = (bf16[24,128]{1,0:T(8,128)(2,1)S(1)}, bf16[24,128]{1,0:T(8,128)(2,1)}, u32[]{:S(2)}) copy-start(bf16[24,128]{1,0:T(8,128)(2,1)} %pack.1) | copy-start | bytes 18436
  17.9 24.1 %copy-start.6 = (s32[197,197]{1,0:T(8,128)S(1)}, s32[197,197]{1,0:T(8,128)}, u32[]{:S(2)}) copy-start(s32[197,197]{1,0:T(8,128)} %param.23) | copy-start | bytes 465712
  25.9 15.3 %all-to-all-start = ((bf16[32,24,128]{2,1,0:T(8,128)(2,1)}), bf16[32,24,128]{2,1,0:T(8,128)(2,1)S(1)}, u32[]{:S(2)}, u32[]{:S(2)}) async-start(bf16[32,24,128]{2,1,0:T(8,128)(2,1)} %broadcast_in_dim.82), calls=%async_computation | async-start | bytes 393216 | tf_op jit(solution)/shard_map/all_to_all | solution.py:1044
  29.8 10.5 %collective-permute-start.1 = (bf16[48,2304]{1,0:T(8,128)(2,1)S(1)}, bf16[48,2304]{1,0:T(8,128)(2,1)S(1)}, u32[]{:S(2)}, u32[]{:S(2)}) collective-permute-start(bf16[48,2304]{1,0:T(8,128)(2,1)S(1)} %pad_maximum_fusion.4), channel_id=1, source_target_pairs={{0,4},{1,9},{2,6},{3,11},{4,0},{5,13},{6,2},{7,15},{8,12},{9,1},{1... | collective-permute-start | bytes 663560 | tf_op jit(solution)/shard_map/ppermute | solution.py:75
  41.2 1.7 copy-start.4
  41.3 15.3 %collective-permute-start.2 = (bf16[96,2304]{1,0:T(8,128)(2,1)S(1)}, bf16[96,2304]{1,0:T(8,128)(2,1)S(1)}, u32[]{:S(2)}, u32[]{:S(2)}) collective-permute-start(bf16[96,2304]{1,0:T(8,128)(2,1)S(1)} %pad_maximum_fusion.1), channel_id=1, source_target_pairs={{0,16},{1,3},{2,18},{3,1},{4,20},{5,7},{6,22},{7,5},{8,24},{9,11},... | collective-permute-start | bytes 1327112 | tf_op jit(solution)/shard_map/ppermute | solution.py:75
  56.6 13.1 %collective-permute-start.3 = (bf16[192,2304]{1,0:T(8,128)(2,1)S(1)}, bf16[192,2304]{1,0:T(8,128)(2,1)S(1)}, u32[]{:S(2)}, u32[]{:S(2)}) collective-permute-start(bf16[192,2304]{1,0:T(8,128)(2,1)S(1)} %pad_maximum_fusion), channel_id=1, source_target_pairs={{0,2},{1,17},{2,0},{3,19},{4,6},{5,21},{6,4},{7,23},{8,10},{9,25},... | collective-permute-start | bytes 2654216 | tf_op jit(solution)/shard_map/ppermute | solution.py:75
  69.8 3.8 %copy-start = (bf16[384,2304]{1,0:T(8,128)(2,1)}, bf16[384,2304]{1,0:T(8,128)(2,1)S(1)}, u32[]{:S(2)}) copy-start(bf16[384,2304]{1,0:T(8,128)(2,1)S(1)} %constant_dynamic-update-slice_fusion) | copy-start | bytes 5308420
  69.8 3.8 %collective-permute-start.4 = (bf16[384,2304]{1,0:T(8,128)(2,1)S(1)}, bf16[384,2304]{1,0:T(8,128)(2,1)S(1)}, u32[]{:S(2)}, u32[]{:S(2)}) collective-permute-start(bf16[384,2304]{1,0:T(8,128)(2,1)S(1)} %constant_dynamic-update-slice_fusion), channel_id=1, source_target_pairs={{0,1},{1,0},{2,3},{3,2},{4,5},{5,4},{6,7},{7,6},{8,9},{9,8},{10,11... | collective-permute-start | bytes 5308424 | tf_op jit(solution)/shard_map/ppermute | solution.py:75
  73.5 1.2 copy-start.2
  158.6 9.2 %collective-permute-start.5 = (bf16[2,384,3456]{2,1,0:T(8,128)(2,1)}, bf16[2,384,3456]{2,1,0:T(8,128)(2,1)}, u32[]{:S(2)}, u32[]{:S(2)}) collective-permute-start(bf16[2,384,3456]{2,1,0:T(8,128)(2,1)} %get-tuple-element.94), channel_id=1, source_target_pairs={{0,1},{1,0},{2,3},{3,2},{4,5},{5,4},{6,7},{7,6},{8,9},{9,8},{10,11... | collective-permute-start | bytes 15925256 | tf_op jit(solution)/shard_map/ppermute | solution.py:75
  172.4 34.3 %collective-permute-start.8 = (bf16[2,192,3456]{2,1,0:T(8,128)(2,1)}, bf16[2,192,3456]{2,1,0:T(8,128)(2,1)S(1)}, u32[]{:S(2)}, u32[]{:S(2)}) collective-permute-start(bf16[2,192,3456]{2,1,0:T(8,128)(2,1)} %add_convert_fusion), channel_id=1, source_target_pairs={{0,2},{1,17},{2,0},{3,19},{4,6},{5,21},{6,4},{7,23},{8,10},{9,25},... | collective-permute-start | bytes 7962632 | tf_op jit(solution)/shard_map/ppermute | solution.py:75
  189.2 4.0 %collective-permute-start.6 = (bf16[384,2304]{1,0:T(8,128)(2,1)}, bf16[384,2304]{1,0:T(8,128)(2,1)}, u32[]{:S(2)}, u32[]{:S(2)}) collective-permute-start(bf16[384,2304]{1,0:T(8,128)(2,1)} %get-tuple-element.101), channel_id=1, source_target_pairs={{0,1},{1,0},{2,3},{3,2},{4,5},{5,4},{6,7},{7,6},{8,9},{9,8},{10,11... | collective-permute-start | bytes 5308424 | tf_op jit(solution)/shard_map/ppermute | solution.py:75
  195.7 22.7 %collective-permute-start.7 = (bf16[192,2304]{1,0:T(8,128)(2,1)}, bf16[192,2304]{1,0:T(8,128)(2,1)S(1)}, u32[]{:S(2)}, u32[]{:S(2)}) collective-permute-start(bf16[192,2304]{1,0:T(8,128)(2,1)} %add_convert_fusion.2), channel_id=1, source_target_pairs={{0,4},{1,9},{2,6},{3,11},{4,0},{5,13},{6,2},{7,15},{8,12},{9,1},{1... | collective-permute-start | bytes 2654216 | tf_op jit(solution)/shard_map/ppermute | solution.py:75
  206.7 3.9 %copy-start.5 = (f32[32,4,24]{2,1,0:T(4,128)S(1)}, f32[32,4,24]{2,1,0:T(4,128)}, u32[]{:S(2)}) copy-start(f32[32,4,24]{2,1,0:T(4,128)} %reshape_squeeze.3) | copy-start | bytes 36868
  206.7 4.6 %copy-start.9 = (f32[16,768]{1,0:T(8,128)S(1)}, f32[16,768]{1,0:T(8,128)}, u32[]{:S(2)}) copy-start(f32[16,768]{1,0:T(8,128)} %get-tuple-element.121) | copy-start | bytes 147460
  206.7 4.5 %copy-start.10 = (f32[16,768]{1,0:T(8,128)S(1)}, f32[16,768]{1,0:T(8,128)}, u32[]{:S(2)}) copy-start(f32[16,768]{1,0:T(8,128)} %get-tuple-element.120) | copy-start | bytes 147460
  210.0 19.0 %collective-permute-start.10 = (bf16[2,96,3456]{2,1,0:T(8,128)(2,1)}, bf16[2,96,3456]{2,1,0:T(8,128)(2,1)}, u32[]{:S(2)}, u32[]{:S(2)}) collective-permute-start(bf16[2,96,3456]{2,1,0:T(8,128)(2,1)} %add_convert_fusion.1), channel_id=1, source_target_pairs={{0,16},{1,3},{2,18},{3,1},{4,20},{5,7},{6,22},{7,5},{8,24},{9,11},... | collective-permute-start | bytes 3981320 | tf_op jit(solution)/shard_map/ppermute | solution.py:75
  218.5 15.7 %copy-start.3 = (bf16[192,2304]{1,0:T(8,128)(2,1)}, bf16[192,2304]{1,0:T(8,128)(2,1)S(1)}, u32[]{:S(2)}) copy-start(bf16[192,2304]{1,0:T(8,128)(2,1)S(1)} %collective-permute-done.7) | copy-start | bytes 2654212
  220.1 14.1 %collective-permute-start.9 = (bf16[96,2304]{1,0:T(8,128)(2,1)S(1)}, bf16[96,2304]{1,0:T(8,128)(2,1)}, u32[]{:S(2)}, u32[]{:S(2)}) collective-permute-start(bf16[96,2304]{1,0:T(8,128)(2,1)S(1)} %add_convert_fusion.4), channel_id=1, source_target_pairs={{0,8},{1,5},{2,10},{3,7},{4,12},{5,1},{6,14},{7,3},{8,0},{9,13},{1... | collective-permute-start | bytes 1327112 | tf_op jit(solution)/shard_map/ppermute | solution.py:75
  229.0 7.2 %copy-start.7 = (f32[16,768]{1,0:T(8,128)S(1)}, f32[16,768]{1,0:T(8,128)}, u32[]{:S(2)}) copy-start(f32[16,768]{1,0:T(8,128)} %table_grad.2) | copy-start | bytes 147460
  229.0 7.2 %copy-start.8 = (f32[16,768]{1,0:T(8,128)S(1)}, f32[16,768]{1,0:T(8,128)}, u32[]{:S(2)}) copy-start(f32[16,768]{1,0:T(8,128)} %table_grad.3) | copy-start | bytes 147460
  231.7 21.5 %collective-permute-start.12 = (bf16[2,48,3456]{2,1,0:T(8,128)(2,1)}, bf16[2,48,3456]{2,1,0:T(8,128)(2,1)}, u32[]{:S(2)}, u32[]{:S(2)}) collective-permute-start(bf16[2,48,3456]{2,1,0:T(8,128)(2,1)} %add_convert_fusion.3), channel_id=1, source_target_pairs={{0,4},{1,9},{2,6},{3,11},{4,0},{5,13},{6,2},{7,15},{8,12},{9,1},{1... | collective-permute-start | bytes 1990664 | tf_op jit(solution)/shard_map/ppermute | solution.py:75
  238.6 13.1 %all-to-all-start.1 = ((f32[32,1,624]{2,1,0:T(1,128)}), f32[32,1,624]{2,1,0:T(1,128)S(1)}, u32[]{:S(2)}, u32[]{:S(2)}) async-start(f32[32,1,624]{2,1,0:T(1,128)} %reshape.169), calls=%async_computation.1 | async-start | bytes 163840 | tf_op jit(solution)/shard_map/all_to_all | solution.py:1101
  242.0 14.2 %collective-permute-start.11 = (bf16[48,2304]{1,0:T(8,128)(2,1)}, bf16[48,2304]{1,0:T(8,128)(2,1)}, u32[]{:S(2)}, u32[]{:S(2)}) collective-permute-start(bf16[48,2304]{1,0:T(8,128)(2,1)} %add_convert_fusion.6), channel_id=1, source_target_pairs={{0,2},{1,17},{2,0},{3,19},{4,6},{5,21},{6,4},{7,23},{8,10},{9,25},... | collective-permute-start | bytes 663560 | tf_op jit(solution)/shard_map/ppermute | solution.py:75
  255.5 11.8 %collective-permute-start.14 = (bf16[2,24,3456]{2,1,0:T(8,128)(2,1)}, bf16[2,24,3456]{2,1,0:T(8,128)(2,1)S(1)}, u32[]{:S(2)}, u32[]{:S(2)}) collective-permute-start(bf16[2,24,3456]{2,1,0:T(8,128)(2,1)} %add_convert_fusion.5), channel_id=1, source_target_pairs={{0,8},{1,5},{2,10},{3,7},{4,12},{5,1},{6,14},{7,3},{8,0},{9,13},{1... | collective-permute-start | bytes 995336 | tf_op jit(solution)/shard_map/ppermute | solution.py:75
  257.9 11.7 %collective-permute-start.13 = (bf16[24,2304]{1,0:T(8,128)(2,1)}, bf16[24,2304]{1,0:T(8,128)(2,1)S(1)}, u32[]{:S(2)}, u32[]{:S(2)}) collective-permute-start(bf16[24,2304]{1,0:T(8,128)(2,1)} %add_convert_fusion.7), channel_id=1, source_target_pairs={{0,16},{1,3},{2,18},{3,1},{4,20},{5,7},{6,22},{7,5},{8,24},{9,11},... | collective-permute-start | bytes 331784 | tf_op jit(solution)/shard_map/ppermute | solution.py:75
Sparse Core Ops, SparseCore 0:
  10.9 98.7 all-gather.1
